TPU v7x, 32 devices: a whole 2x2x4 slice. The times are simulated.
32 devices in a mesh: row: 16 (over z, x, core), col: 2 (over y).
Axes of the slice: x: 2, y: 2, z: 4, core: 2. Of those that a mesh axis runs over, the one named last changes fastest.
Arguments:
- queries: bfloat16 [16384, 256], P(('row', 'col')), may hold values from -36 to 36
- key_rows: bfloat16 [16384, 128], P(('row', 'col')), may hold values from -16 to 16
- value_rows: bfloat16 [16384, 128], P(('row', 'col')), may hold values from -6 to 6
- out_grad: bfloat16 [16384, 256], P(('row', 'col')), may hold values from -6 to 6
- link_mask: int32 [32, 5], P(('row', 'col')), may hold values 0 or 1
Outputs:
- attention_out: bfloat16 [16384, 256], P(('row', 'col'))
- query_grad: bfloat16 [16384, 256], P(('row', 'col'))
- key_grad: bfloat16 [16384, 128], P(('row', 'col'))
- value_grad: bfloat16 [16384, 128], P(('row', 'col'))
All inputs are finite; a program needn't handle non-finite values. No bound on the sum of `link_mask` on one device may be relied on, other than what follows from the above.
Results may differ from a plain program's by a relative error of at most 0.025.
Values may be sent and summed in bfloat16 or wider, within the bound.
No kernel may reach another device: no remote copies, remote signals or barrier semaphores. Data moves between devices by JAX's collectives and lax.ppermute only.
A program may use at most 64 MiB of HBM per device.

v0:
```python
import math

import jax
import jax.numpy as jnp
from jax import lax
from jax.sharding import PartitionSpec as P

scale_eps = 1e-06


def shifted(value, axis, steps):
    count = lax.axis_size(axis)
    leading, last = (max(0, -steps), min(count, count - steps))
    return lax.ppermute(value, axis, [(source, source + steps) for source in range(leading, last)])


def quantize(values):
    largest = jnp.max(jnp.abs(values), axis=-1)
    scales = (largest + scale_eps).astype(jnp.bfloat16)
    scaled = values * (127.0 / scales.astype(jnp.float32))[..., None]
    codes = jnp.clip(jnp.floor(scaled + 0.5), -127.0, 127.0).astype(jnp.bfloat16)
    return (codes, scales)


def dequantize(codes, scales):
    return (codes.astype(jnp.float32) * (scales.astype(jnp.float32) / 127.0)[..., None]).astype(
        jnp.bfloat16
    )


def score_block(query_codes, query_scales, key_codes, key_scales):
    head_size = key_codes.shape[-1]
    factor = 1.0 / (127.0 * 127.0 * math.sqrt(head_size))
    raw = jnp.einsum("thc,uc->htu", query_codes, key_codes, preferred_element_type=jnp.float32)
    row_factor = jnp.transpose(query_scales.astype(jnp.float32) * factor)
    return raw * row_factor[:, :, None] * key_scales.astype(jnp.float32)[None, None, :]


def fetch_keys(bundle, distance):
    return shifted((bundle[0], bundle[1], bundle[2]), ("row", "col"), distance)


def return_grads(partials):
    levels_count = len(partials)
    running = partials[levels_count - 1]
    distances = [2**level for level in range(levels_count - 2, -1, -1)] + [1]
    extras = [partials[level] for level in range(levels_count - 2, -1, -1)] + [None]
    for distance, extra in zip(distances, extras):
        running = shifted(running, ("row", "col"), -distance)
        if extra is not None:
            running = (running[0] + extra[0], running[1] + extra[1])
    return running


def local(queries, key_rows, value_rows, out_grad, link_mask):
    tokens_dev = queries.shape[0]
    head_size = key_rows.shape[1]
    heads_count = queries.shape[1] // head_size
    levels_count = link_mask.shape[1]
    score_scale = 1.0 / math.sqrt(head_size)
    query_float = queries.astype(jnp.float32).reshape(tokens_dev, heads_count, head_size)
    query_codes, query_scales = quantize(query_float)
    query_hat = dequantize(query_codes, query_scales)
    key_codes, key_scales = quantize(key_rows.astype(jnp.float32))
    grad_three = out_grad.reshape(tokens_dev, heads_count, head_size)
    grad_float = grad_three.astype(jnp.float32)
    block_id = lax.axis_index(("row", "col"))
    positions = jnp.arange(tokens_dev, dtype=jnp.int32)
    causal = (positions[None, :] <= positions[:, None])[None, :, :]
    sources = [((key_codes, key_scales, value_rows), causal)]
    for level in range(levels_count):
        distance = 2**level
        fetched = fetch_keys((key_codes, key_scales, value_rows), distance)
        allowed = jnp.logical_and(block_id >= distance, link_mask[0, level] == 1)
        sources.append((fetched, allowed))

    def masked_scores(bundle, allowed):
        return jnp.where(
            allowed, score_block(query_codes, query_scales, bundle[0], bundle[1]), -jnp.inf
        )

    row_top = None
    for bundle, allowed in sources:
        current = jnp.max(masked_scores(bundle, allowed), axis=2)
        row_top = current if row_top is None else jnp.maximum(row_top, current)
    total = jnp.zeros((heads_count, tokens_dev), jnp.float32)
    mixed = jnp.zeros((tokens_dev, heads_count, head_size), jnp.float32)
    for bundle, allowed in sources:
        weights = jnp.exp(masked_scores(bundle, allowed) - row_top[:, :, None])
        total = total + jnp.sum(weights, axis=2)
        mixed = mixed + jnp.einsum(
            "htu,uc->thc",
            weights.astype(jnp.bfloat16),
            bundle[2],
            preferred_element_type=jnp.float32,
        )
    attended = (mixed / jnp.transpose(total)[:, :, None]).astype(jnp.bfloat16)
    delta = jnp.sum(grad_float * attended.astype(jnp.float32), axis=2)
    query_sum = jnp.zeros((tokens_dev, heads_count, head_size), jnp.float32)
    partials = []
    own_part = None
    for position, (bundle, allowed) in enumerate(sources):
        weights = jnp.exp(masked_scores(bundle, allowed) - row_top[:, :, None])
        probs = weights / total[:, :, None]
        grad_probs = jnp.einsum(
            "thc,uc->htu", grad_three, bundle[2], preferred_element_type=jnp.float32
        )
        grad_scores = (
            probs * (grad_probs - jnp.transpose(delta)[:, :, None]) * score_scale
        ).astype(jnp.bfloat16)
        key_hat = dequantize(bundle[0], bundle[1])
        query_sum = query_sum + jnp.einsum(
            "htu,uc->thc", grad_scores, key_hat, preferred_element_type=jnp.float32
        )
        key_part = jnp.einsum(
            "htu,thc->uc", grad_scores, query_hat, preferred_element_type=jnp.float32
        )
        value_part = jnp.einsum(
            "htu,thc->uc",
            probs.astype(jnp.bfloat16),
            grad_three,
            preferred_element_type=jnp.float32,
        )
        if position == 0:
            own_part = (key_part, value_part)
        else:
            partials.append((key_part, value_part))
    key_back, value_back = return_grads(partials)
    attention_out = attended.reshape(tokens_dev, heads_count * head_size)
    query_grad = query_sum.astype(jnp.bfloat16).reshape(tokens_dev, heads_count * head_size)
    key_grad = (own_part[0] + key_back).astype(jnp.bfloat16)
    value_grad = (own_part[1] + value_back).astype(jnp.bfloat16)
    return (attention_out, query_grad, key_grad, value_grad)


def solution(mesh):
    return jax.shard_map(
        local,
        mesh=mesh,
        in_specs=(
            P(("row", "col"), None),
            P(("row", "col"), None),
            P(("row", "col"), None),
            P(("row", "col"), None),
            P(("row", "col"), None),
        ),
        out_specs=(
            P(("row", "col"), None),
            P(("row", "col"), None),
            P(("row", "col"), None),
            P(("row", "col"), None),
        ),
        check_vma=False,
    )
```

profile of v0, /device:TPU:0, one launch (start us, length us, event | category | flops | bytes accessed | tf_op | source)
XLA Modules:
  0.0 146.4 jit_solution(10082554455150450813)
XLA Ops:
  4.0 4.9 %collective-permute-start.4 = (bf16[512,128]{1,0:T(8,128)(2,1)S(1)}, bf16[512,128]{1,0:T(8,128)(2,1)S(1)}, u32[]{:S(2)}, u32[]{:S(2)}) collective-permute-start(bf16[512,128]{1,0:T(8,128)(2,1)S(1)} %fusion.71), channel_id=1, source_target_pairs={{0,4},{1,5},{2,6},{3,7},{4,8},{5,9},{6,10},{7,11},{8,12},{9,13},{1... | collective-permute-start | bytes 393224 | tf_op jit(solution)/shard_map/ppermute | solution.py:14
  10.3 5.0 %collective-permute-start.8 = (bf16[512,128]{1,0:T(8,128)(2,1)S(1)}, bf16[512,128]{1,0:T(8,128)(2,1)S(1)}, u32[]{:S(2)}, u32[]{:S(2)}) collective-permute-start(bf16[512,128]{1,0:T(8,128)(2,1)S(1)} %fusion.71), channel_id=1, source_target_pairs={{0,16},{1,17},{2,18},{3,19},{4,20},{5,21},{6,22},{7,23},{8,24},{9,... | collective-permute-start | bytes 393224 | tf_op jit(solution)/shard_map/ppermute | solution.py:14
  15.3 3.5 %collective-permute-start.6 = (bf16[512,128]{1,0:T(8,128)(2,1)S(1)}, bf16[512,128]{1,0:T(8,128)(2,1)S(1)}, u32[]{:S(2)}, u32[]{:S(2)}) collective-permute-start(bf16[512,128]{1,0:T(8,128)(2,1)S(1)} %fusion.71), channel_id=1, source_target_pairs={{0,8},{1,9},{2,10},{3,11},{4,12},{5,13},{6,14},{7,15},{8,16},{9,17... | collective-permute-start | bytes 393224 | tf_op jit(solution)/shard_map/ppermute | solution.py:14
  18.8 4.0 %collective-permute-start.1 = (bf16[512]{0:T(512)(128)(2,1)}, bf16[512]{0:T(512)(128)(2,1)}, u32[]{:S(2)}, u32[]{:S(2)}) collective-permute-start(bf16[512]{0:T(512)(128)(2,1)} %get-tuple-element.32), channel_id=1, source_target_pairs={{0,1},{1,2},{2,3},{3,4},{4,5},{5,6},{6,7},{7,8},{8,9},{9,10},{10,1... | collective-permute-start | bytes 3080 | tf_op jit(solution)/shard_map/ppermute | solution.py:14
  34.3 3.5 %collective-permute-start.5 = (bf16[512]{0:T(512)(128)(2,1)}, bf16[512]{0:T(512)(128)(2,1)S(1)}, u32[]{:S(2)}, u32[]{:S(2)}) collective-permute-start(bf16[512]{0:T(512)(128)(2,1)} %get-tuple-element.32), channel_id=1, source_target_pairs={{0,4},{1,5},{2,6},{3,7},{4,8},{5,9},{6,10},{7,11},{8,12},{9,13},{1... | collective-permute-start | bytes 3080 | tf_op jit(solution)/shard_map/ppermute | solution.py:14
  39.3 6.6 %collective-permute-start.7 = (bf16[512]{0:T(512)(128)(2,1)}, bf16[512]{0:T(512)(128)(2,1)S(1)}, u32[]{:S(2)}, u32[]{:S(2)}) collective-permute-start(bf16[512]{0:T(512)(128)(2,1)} %get-tuple-element.32), channel_id=1, source_target_pairs={{0,8},{1,9},{2,10},{3,11},{4,12},{5,13},{6,14},{7,15},{8,16},{9,17... | collective-permute-start | bytes 3080 | tf_op jit(solution)/shard_map/ppermute | solution.py:14
  47.4 3.6 %collective-permute-start.9 = (bf16[512]{0:T(512)(128)(2,1)}, bf16[512]{0:T(512)(128)(2,1)S(1)}, u32[]{:S(2)}, u32[]{:S(2)}) collective-permute-start(bf16[512]{0:T(512)(128)(2,1)} %get-tuple-element.32), channel_id=1, source_target_pairs={{0,16},{1,17},{2,18},{3,19},{4,20},{5,21},{6,22},{7,23},{8,24},{9,... | collective-permute-start | bytes 3080 | tf_op jit(solution)/shard_map/ppermute | solution.py:14
  52.5 2.0 %collective-permute-start = (bf16[512,128]{1,0:T(8,128)(2,1)S(1)}, bf16[512,128]{1,0:T(8,128)(2,1)S(1)}, u32[]{:S(2)}, u32[]{:S(2)}) collective-permute-start(bf16[512,128]{1,0:T(8,128)(2,1)S(1)} %fusion.71), channel_id=1, source_target_pairs={{0,1},{1,2},{2,3},{3,4},{4,5},{5,6},{6,7},{7,8},{8,9},{9,10},{10,1... | collective-permute-start | bytes 393224 | tf_op jit(solution)/shard_map/ppermute | solution.py:14
  54.6 1.9 %collective-permute-start.10 = (bf16[512,128]{0,1:T(8,128)(2,1)S(1)}, bf16[512,128]{0,1:T(8,128)(2,1)S(1)}, u32[]{:S(2)}, u32[]{:S(2)}) collective-permute-start(bf16[512,128]{0,1:T(8,128)(2,1)S(1)} %copy.163), channel_id=1, source_target_pairs={{0,1},{1,2},{2,3},{3,4},{4,5},{5,6},{6,7},{7,8},{8,9},{9,10},{10,1... | collective-permute-start | bytes 393224 | tf_op jit(solution)/shard_map/ppermute | solution.py:14
  57.0 1.6 %collective-permute-start.12 = (bf16[512,128]{0,1:T(8,128)(2,1)S(1)}, bf16[512,128]{0,1:T(8,128)(2,1)S(1)}, u32[]{:S(2)}, u32[]{:S(2)}) collective-permute-start(bf16[512,128]{0,1:T(8,128)(2,1)S(1)} %copy.163), channel_id=1, source_target_pairs={{0,4},{1,5},{2,6},{3,7},{4,8},{5,9},{6,10},{7,11},{8,12},{9,13},{1... | collective-permute-start | bytes 393224 | tf_op jit(solution)/shard_map/ppermute | solution.py:14
  59.0 2.2 %collective-permute-start.13 = (bf16[512,128]{0,1:T(8,128)(2,1)S(1)}, bf16[512,128]{0,1:T(8,128)(2,1)S(1)}, u32[]{:S(2)}, u32[]{:S(2)}) collective-permute-start(bf16[512,128]{0,1:T(8,128)(2,1)S(1)} %copy.163), channel_id=1, source_target_pairs={{0,8},{1,9},{2,10},{3,11},{4,12},{5,13},{6,14},{7,15},{8,16},{9,17... | collective-permute-start | bytes 393224 | tf_op jit(solution)/shard_map/ppermute | solution.py:14
  61.8 5.1 %collective-permute-start.14 = (bf16[512,128]{0,1:T(8,128)(2,1)S(1)}, bf16[512,128]{0,1:T(8,128)(2,1)S(1)}, u32[]{:S(2)}, u32[]{:S(2)}) collective-permute-start(bf16[512,128]{0,1:T(8,128)(2,1)S(1)} %copy.163), channel_id=1, source_target_pairs={{0,16},{1,17},{2,18},{3,19},{4,20},{5,21},{6,22},{7,23},{8,24},{9,... | collective-permute-start | bytes 393224 | tf_op jit(solution)/shard_map/ppermute | solution.py:14
  67.3 3.9 %collective-permute-start.11 = (bf16[512,128]{0,1:T(8,128)(2,1)S(1)}, bf16[512,128]{0,1:T(8,128)(2,1)S(1)}, u32[]{:S(2)}, u32[]{:S(2)}) collective-permute-start(bf16[512,128]{0,1:T(8,128)(2,1)S(1)} %copy.163), channel_id=1, source_target_pairs={{0,2},{1,3},{2,4},{3,5},{4,6},{5,7},{6,8},{7,9},{8,10},{9,11},{10,... | collective-permute-start | bytes 393224 | tf_op jit(solution)/shard_map/ppermute | solution.py:14
  71.2 2.1 %fusion.31 = (f32[2,512]{1,0:T(2,128)S(1)}, f32[2,512]{1,0:T(2,128)S(1)}, f32[2,512]{1,0:T(2,128)S(1)}, f32[2,512]{1,0:T(2,128)S(1)}, f32[2,512]{1,0:T(2,128)S(1...) fusion(f32[512]{0:T(512)S(1)} %convert_element_type.236, f32[2,512]{1,0:T(2,128)S(1)} %get-tuple-element.34, ...), kind=kOutput, calls=%fused_computation.49 | convolution fusion | flops 146794496 | bytes 13279237 | tf_op jit(solution)/shard_map/thc,uc->htu/dot_general | solution.py:34
  73.9 2.8 %fusion.116 = (f32[2,512]{1,0:T(2,128)S(1)}, f32[2,512]{1,0:T(2,128)S(1)}, f32[2,512]{1,0:T(2,128)S(1)}, f32[2,512]{1,0:T(2,128)S(1)}, f32[2,512]{1,0:T(2,128)S(1)}) fusion(f32[2,512]{1,0:T(2,128)S(1)} %maximum_maximum_fusion, f32[512]{0:T(512)S(1)} %convert_element_type.236, f32[2,512]{1,0:T(2,128)S(1)} %get-tuple-element.34, ...), kind=kLoop, calls=%fused_computation.177 | loop fusion | flops 13102080 | bytes 10786820 | tf_op jit(solution)/shard_map/reduce_sum | solution.py:90
  101.6 7.7 %collective-permute-done.21 = f32[512,128]{1,0:T(8,128)S(1)} collective-permute-done((f32[512,128]{1,0:T(8,128)S(1)}, f32[512,128]{1,0:T(8,128)S(1)}, u32[]{:S(2)}, u32[]{:S(2)}) %collective-permute-start.21) | collective-permute-done | bytes 262176 | tf_op jit(solution)/shard_map/ppermute | solution.py:14
  109.4 1.6 %collective-permute-start.22 = (f32[512,128]{1,0:T(8,128)S(1)}, f32[512,128]{1,0:T(8,128)S(1)}, u32[]{:S(2)}, u32[]{:S(2)}) collective-permute-start(f32[512,128]{1,0:T(8,128)S(1)} %add.201), channel_id=1, source_target_pairs={{2,0},{3,1},{4,2},{5,3},{6,4},{7,5},{8,6},{9,7},{10,8},{11,9},{12,... | collective-permute-start | bytes 786440 | tf_op jit(solution)/shard_map/ppermute | solution.py:14
  111.5 2.5 %collective-permute-done.16 = f32[512,128]{1,0:T(8,128)S(1)} collective-permute-done((f32[512,128]{1,0:T(8,128)S(1)}, f32[512,128]{1,0:T(8,128)S(1)}, u32[]{:S(2)}, u32[]{:S(2)}) %collective-permute-start.16) | collective-permute-done | bytes 262176 | tf_op jit(solution)/shard_map/ppermute | solution.py:14
  119.9 4.6 %collective-permute-done.23 = f32[512,128]{1,0:T(8,128)S(1)} collective-permute-done((f32[512,128]{1,0:T(8,128)S(1)}, f32[512,128]{1,0:T(8,128)S(1)}, u32[]{:S(2)}, u32[]{:S(2)}) %collective-permute-start.23) | collective-permute-done | bytes 262176 | tf_op jit(solution)/shard_map/ppermute | solution.py:14
  127.7 1.8 %copy.204 = bf16[512,256]{1,0:T(8,128)(2,1)} copy(bf16[512,256]{0,1:T(8,128)(2,1)} %bitcast.333) | data formatting | bytes 524288
  129.5 1.8 %copy.203 = bf16[512,256]{1,0:T(8,128)(2,1)} copy(bf16[512,256]{0,1:T(8,128)(2,1)} %bitcast.346) | data formatting | bytes 524288
  134.2 4.0 %collective-permute-done.24 = f32[512,128]{1,0:T(8,128)} collective-permute-done((f32[512,128]{1,0:T(8,128)}, f32[512,128]{1,0:T(8,128)}, u32[]{:S(2)}, u32[]{:S(2)}) %collective-permute-start.24) | collective-permute-done | bytes 262176 | tf_op jit(solution)/shard_map/ppermute | solution.py:14
  138.3 2.5 %fusion.64 = bf16[512,128]{1,0:T(8,128)(2,1)} fusion(f32[512,128]{1,0:T(8,128)} %collective-permute-done.24, bf16[512,2,128]{0,2,1:T(8,128)(2,1)S(1)} %bitcast.345, f32[2,512]{1,0:T(2,128)S(1)} %copy-done.19, f32[512,512,2]{1,0,2:T(8,128)S(1)} %fusion.107, f32[2,512]{1,0:T(2,128)S(1)} %maximum_maximum_fusion, f32[512]{0:T(512)S(1)} %copy-done.16, ...), kind=kOutput, calls=%fused_computation.106 | convolution fusion | flops 137494528 | bytes 3028992 | tf_op jit(solution)/shard_map/htu,thc->uc/dot_general | solution.py:118
  140.8 5.0 %collective-permute-done.19 = f32[512,128]{1,0:T(8,128)S(1)} collective-permute-done((f32[512,128]{1,0:T(8,128)S(1)}, f32[512,128]{1,0:T(8,128)S(1)}, u32[]{:S(2)}, u32[]{:S(2)}) %collective-permute-start.19) | collective-permute-done | bytes 262176 | tf_op jit(solution)/shard_map/ppermute | solution.py:14
  (139 shorter events, 57.5 us)
Async XLA Ops:
  4.0 50.6 %collective-permute-start.4 = (bf16[512,128]{1,0:T(8,128)(2,1)S(1)}, bf16[512,128]{1,0:T(8,128)(2,1)S(1)}, u32[]{:S(2)}, u32[]{:S(2)}) collective-permute-start(bf16[512,128]{1,0:T(8,128)(2,1)S(1)} %fusion.71), channel_id=1, source_target_pairs={{0,4},{1,5},{2,6},{3,7},{4,8},{5,9},{6,10},{7,11},{8,12},{9,13},{1... | collective-permute-start | bytes 393224 | tf_op jit(solution)/shard_map/ppermute | solution.py:14
  8.9 48.1 %collective-permute-start.2 = (bf16[512,128]{1,0:T(8,128)(2,1)S(1)}, bf16[512,128]{1,0:T(8,128)(2,1)S(1)}, u32[]{:S(2)}, u32[]{:S(2)}) collective-permute-start(bf16[512,128]{1,0:T(8,128)(2,1)S(1)} %fusion.71), channel_id=1, source_target_pairs={{0,2},{1,3},{2,4},{3,5},{4,6},{5,7},{6,8},{7,9},{8,10},{9,11},{10,... | collective-permute-start | bytes 393224 | tf_op jit(solution)/shard_map/ppermute | solution.py:14
  10.3 48.7 %collective-permute-start.8 = (bf16[512,128]{1,0:T(8,128)(2,1)S(1)}, bf16[512,128]{1,0:T(8,128)(2,1)S(1)}, u32[]{:S(2)}, u32[]{:S(2)}) collective-permute-start(bf16[512,128]{1,0:T(8,128)(2,1)S(1)} %fusion.71), channel_id=1, source_target_pairs={{0,16},{1,17},{2,18},{3,19},{4,20},{5,21},{6,22},{7,23},{8,24},{9,... | collective-permute-start | bytes 393224 | tf_op jit(solution)/shard_map/ppermute | solution.py:14
  15.3 46.4 %collective-permute-start.6 = (bf16[512,128]{1,0:T(8,128)(2,1)S(1)}, bf16[512,128]{1,0:T(8,128)(2,1)S(1)}, u32[]{:S(2)}, u32[]{:S(2)}) collective-permute-start(bf16[512,128]{1,0:T(8,128)(2,1)S(1)} %fusion.71), channel_id=1, source_target_pairs={{0,8},{1,9},{2,10},{3,11},{4,12},{5,13},{6,14},{7,15},{8,16},{9,17... | collective-permute-start | bytes 393224 | tf_op jit(solution)/shard_map/ppermute | solution.py:14
  18.8 13.1 %collective-permute-start.1 = (bf16[512]{0:T(512)(128)(2,1)}, bf16[512]{0:T(512)(128)(2,1)}, u32[]{:S(2)}, u32[]{:S(2)}) collective-permute-start(bf16[512]{0:T(512)(128)(2,1)} %get-tuple-element.32), channel_id=1, source_target_pairs={{0,1},{1,2},{2,3},{3,4},{4,5},{5,6},{6,7},{7,8},{8,9},{9,10},{10,1... | collective-permute-start | bytes 3080 | tf_op jit(solution)/shard_map/ppermute | solution.py:14
  34.3 5.0 %collective-permute-start.5 = (bf16[512]{0:T(512)(128)(2,1)}, bf16[512]{0:T(512)(128)(2,1)S(1)}, u32[]{:S(2)}, u32[]{:S(2)}) collective-permute-start(bf16[512]{0:T(512)(128)(2,1)} %get-tuple-element.32), channel_id=1, source_target_pairs={{0,4},{1,5},{2,6},{3,7},{4,8},{5,9},{6,10},{7,11},{8,12},{9,13},{1... | collective-permute-start | bytes 3080 | tf_op jit(solution)/shard_map/ppermute | solution.py:14
  39.3 8.1 %collective-permute-start.7 = (bf16[512]{0:T(512)(128)(2,1)}, bf16[512]{0:T(512)(128)(2,1)S(1)}, u32[]{:S(2)}, u32[]{:S(2)}) collective-permute-start(bf16[512]{0:T(512)(128)(2,1)} %get-tuple-element.32), channel_id=1, source_target_pairs={{0,8},{1,9},{2,10},{3,11},{4,12},{5,13},{6,14},{7,15},{8,16},{9,17... | collective-permute-start | bytes 3080 | tf_op jit(solution)/shard_map/ppermute | solution.py:14
  47.4 5.1 %collective-permute-start.9 = (bf16[512]{0:T(512)(128)(2,1)}, bf16[512]{0:T(512)(128)(2,1)S(1)}, u32[]{:S(2)}, u32[]{:S(2)}) collective-permute-start(bf16[512]{0:T(512)(128)(2,1)} %get-tuple-element.32), channel_id=1, source_target_pairs={{0,16},{1,17},{2,18},{3,19},{4,20},{5,21},{6,22},{7,23},{8,24},{9,... | collective-permute-start | bytes 3080 | tf_op jit(solution)/shard_map/ppermute | solution.py:14
  52.5 14.8 %collective-permute-start = (bf16[512,128]{1,0:T(8,128)(2,1)S(1)}, bf16[512,128]{1,0:T(8,128)(2,1)S(1)}, u32[]{:S(2)}, u32[]{:S(2)}) collective-permute-start(bf16[512,128]{1,0:T(8,128)(2,1)S(1)} %fusion.71), channel_id=1, source_target_pairs={{0,1},{1,2},{2,3},{3,4},{4,5},{5,6},{6,7},{7,8},{8,9},{9,10},{10,1... | collective-permute-start | bytes 393224 | tf_op jit(solution)/shard_map/ppermute | solution.py:14
  54.6 26.1 %collective-permute-start.10 = (bf16[512,128]{0,1:T(8,128)(2,1)S(1)}, bf16[512,128]{0,1:T(8,128)(2,1)S(1)}, u32[]{:S(2)}, u32[]{:S(2)}) collective-permute-start(bf16[512,128]{0,1:T(8,128)(2,1)S(1)} %copy.163), channel_id=1, source_target_pairs={{0,1},{1,2},{2,3},{3,4},{4,5},{5,6},{6,7},{7,8},{8,9},{9,10},{10,1... | collective-permute-start | bytes 393224 | tf_op jit(solution)/shard_map/ppermute | solution.py:14
  57.0 25.9 %collective-permute-start.12 = (bf16[512,128]{0,1:T(8,128)(2,1)S(1)}, bf16[512,128]{0,1:T(8,128)(2,1)S(1)}, u32[]{:S(2)}, u32[]{:S(2)}) collective-permute-start(bf16[512,128]{0,1:T(8,128)(2,1)S(1)} %copy.163), channel_id=1, source_target_pairs={{0,4},{1,5},{2,6},{3,7},{4,8},{5,9},{6,10},{7,11},{8,12},{9,13},{1... | collective-permute-start | bytes 393224 | tf_op jit(solution)/shard_map/ppermute | solution.py:14
  59.0 24.5 %collective-permute-start.13 = (bf16[512,128]{0,1:T(8,128)(2,1)S(1)}, bf16[512,128]{0,1:T(8,128)(2,1)S(1)}, u32[]{:S(2)}, u32[]{:S(2)}) collective-permute-start(bf16[512,128]{0,1:T(8,128)(2,1)S(1)} %copy.163), channel_id=1, source_target_pairs={{0,8},{1,9},{2,10},{3,11},{4,12},{5,13},{6,14},{7,15},{8,16},{9,17... | collective-permute-start | bytes 393224 | tf_op jit(solution)/shard_map/ppermute | solution.py:14
  61.8 22.6 %collective-permute-start.14 = (bf16[512,128]{0,1:T(8,128)(2,1)S(1)}, bf16[512,128]{0,1:T(8,128)(2,1)S(1)}, u32[]{:S(2)}, u32[]{:S(2)}) collective-permute-start(bf16[512,128]{0,1:T(8,128)(2,1)S(1)} %copy.163), channel_id=1, source_target_pairs={{0,16},{1,17},{2,18},{3,19},{4,20},{5,21},{6,22},{7,23},{8,24},{9,... | collective-permute-start | bytes 393224 | tf_op jit(solution)/shard_map/ppermute | solution.py:14
  67.3 17.7 %collective-permute-start.11 = (bf16[512,128]{0,1:T(8,128)(2,1)S(1)}, bf16[512,128]{0,1:T(8,128)(2,1)S(1)}, u32[]{:S(2)}, u32[]{:S(2)}) collective-permute-start(bf16[512,128]{0,1:T(8,128)(2,1)S(1)} %copy.163), channel_id=1, source_target_pairs={{0,2},{1,3},{2,4},{3,5},{4,6},{5,7},{6,8},{7,9},{8,10},{9,11},{10,... | collective-permute-start | bytes 393224 | tf_op jit(solution)/shard_map/ppermute | solution.py:14
  80.6 16.7 %collective-permute-start.20 = (f32[512,128]{1,0:T(8,128)S(1)}, f32[512,128]{1,0:T(8,128)S(1)}, u32[]{:S(2)}, u32[]{:S(2)}) collective-permute-start(f32[512,128]{1,0:T(8,128)S(1)} %convolution_bitcast_fusion.4), channel_id=1, source_target_pairs={{8,0},{9,1},{10,2},{11,3},{12,4},{13,5},{14,6},{15,7},{16,8},{17,9... | collective-permute-start | bytes 786440 | tf_op jit(solution)/shard_map/ppermute | solution.py:14
  89.0 10.7 %collective-permute-start.15 = (f32[512,128]{1,0:T(8,128)S(1)}, f32[512,128]{1,0:T(8,128)S(1)}, u32[]{:S(2)}, u32[]{:S(2)}) collective-permute-start(f32[512,128]{1,0:T(8,128)S(1)} %convolution_bitcast_fusion.10), channel_id=1, source_target_pairs={{8,0},{9,1},{10,2},{11,3},{12,4},{13,5},{14,6},{15,7},{16,8},{17,9... | collective-permute-start | bytes 786440 | tf_op jit(solution)/shard_map/ppermute | solution.py:14
  98.1 11.2 %collective-permute-start.21 = (f32[512,128]{1,0:T(8,128)S(1)}, f32[512,128]{1,0:T(8,128)S(1)}, u32[]{:S(2)}, u32[]{:S(2)}) collective-permute-start(f32[512,128]{1,0:T(8,128)S(1)} %fusion.44), channel_id=1, source_target_pairs={{4,0},{5,1},{6,2},{7,3},{8,4},{9,5},{10,6},{11,7},{12,8},{13,9},{1... | collective-permute-start | bytes 786440 | tf_op jit(solution)/shard_map/ppermute | solution.py:14
  100.3 13.6 %collective-permute-start.16 = (f32[512,128]{1,0:T(8,128)S(1)}, f32[512,128]{1,0:T(8,128)S(1)}, u32[]{:S(2)}, u32[]{:S(2)}) collective-permute-start(f32[512,128]{1,0:T(8,128)S(1)} %fusion.43), channel_id=1, source_target_pairs={{4,0},{5,1},{6,2},{7,3},{8,4},{9,5},{10,6},{11,7},{12,8},{13,9},{1... | collective-permute-start | bytes 786440 | tf_op jit(solution)/shard_map/ppermute | solution.py:14
  109.4 6.0 %collective-permute-start.22 = (f32[512,128]{1,0:T(8,128)S(1)}, f32[512,128]{1,0:T(8,128)S(1)}, u32[]{:S(2)}, u32[]{:S(2)}) collective-permute-start(f32[512,128]{1,0:T(8,128)S(1)} %add.201), channel_id=1, source_target_pairs={{2,0},{3,1},{4,2},{5,3},{6,4},{7,5},{8,6},{9,7},{10,8},{11,9},{12,... | collective-permute-start | bytes 786440 | tf_op jit(solution)/shard_map/ppermute | solution.py:14
  114.0 3.8 %collective-permute-start.17 = (f32[512,128]{1,0:T(8,128)S(1)}, f32[512,128]{1,0:T(8,128)S(1)}, u32[]{:S(2)}, u32[]{:S(2)}) collective-permute-start(f32[512,128]{1,0:T(8,128)S(1)} %add.196), channel_id=1, source_target_pairs={{2,0},{3,1},{4,2},{5,3},{6,4},{7,5},{8,6},{9,7},{10,8},{11,9},{12,... | collective-permute-start | bytes 786440 | tf_op jit(solution)/shard_map/ppermute | solution.py:14
  115.4 9.1 %collective-permute-start.23 = (f32[512,128]{1,0:T(8,128)S(1)}, f32[512,128]{1,0:T(8,128)S(1)}, u32[]{:S(2)}, u32[]{:S(2)}) collective-permute-start(f32[512,128]{1,0:T(8,128)S(1)} %add.202), channel_id=1, source_target_pairs={{1,0},{2,1},{3,2},{4,3},{5,4},{6,5},{7,6},{8,7},{9,8},{10,9},{11,1... | collective-permute-start | bytes 786440 | tf_op jit(solution)/shard_map/ppermute | solution.py:14
  118.6 13.3 %collective-permute-start.18 = (f32[512,128]{1,0:T(8,128)}, f32[512,128]{1,0:T(8,128)}, u32[]{:S(2)}, u32[]{:S(2)}) collective-permute-start(f32[512,128]{1,0:T(8,128)} %add.197), channel_id=1, source_target_pairs={{1,0},{2,1},{3,2},{4,3},{5,4},{6,5},{7,6},{8,7},{9,8},{10,9},{11,1... | collective-permute-start | bytes 786440 | tf_op jit(solution)/shard_map/ppermute | solution.py:14
  125.2 13.1 %collective-permute-start.24 = (f32[512,128]{1,0:T(8,128)}, f32[512,128]{1,0:T(8,128)}, u32[]{:S(2)}, u32[]{:S(2)}) collective-permute-start(f32[512,128]{1,0:T(8,128)} %add.203), channel_id=1, source_target_pairs={{1,0},{2,1},{3,2},{4,3},{5,4},{6,5},{7,6},{8,7},{9,8},{10,9},{11,1... | collective-permute-start | bytes 786440 | tf_op jit(solution)/shard_map/ppermute | solution.py:14
  132.9 12.8 %collective-permute-start.19 = (f32[512,128]{1,0:T(8,128)S(1)}, f32[512,128]{1,0:T(8,128)S(1)}, u32[]{:S(2)}, u32[]{:S(2)}) collective-permute-start(f32[512,128]{1,0:T(8,128)S(1)} %add.198), channel_id=1, source_target_pairs={{1,0},{2,1},{3,2},{4,3},{5,4},{6,5},{7,6},{8,7},{9,8},{10,9},{11,1... | collective-permute-start | bytes 786440 | tf_op jit(solution)/shard_map/ppermute | solution.py:14
  (21 other events, 179.1 us)
where the time goes:
time: 149 us; the launch traced here: 146 us
  starting transfers between devices  64.1 us (43%)
  matrix products  28.3 us (19%)
  waiting for transfers between devices  28.2 us (19%)
  other arithmetic  13 us (9%)
  local copies, waits for them, and re-layouts  8.05 us (5%)
  between operations  4.77 us (3%)
    ppermute x25, starting transfers between devices, shifted(): lax.ppermute(value, axis, [(source, source + steps) for source in range(l...  64.1 us
    ppermute x25, waiting for transfers between devices, shifted(): lax.ppermute(value, axis, [(source, source + steps) for source in range(l...  28.2 us
    unnamed x45, local copies, waits for them, and re-layouts  7.29 us
    dot_general x6, matrix products, local(): jnp.einsum('htu,thc->uc', probs.astype(jnp.bfloat16), grad_three, preferr...  6.06 us
    dot_general x6, matrix products, local(): jnp.einsum('thc,uc->htu', grad_three, bundle[2], preferred_element_type=j...  5.43 us
    dot_general x6, matrix products, local(): jnp.einsum('htu,uc->thc', weights.astype(jnp.bfloat16), bundle[2], prefer...  5.12 us
    dot_general x6, matrix products, score_block(): jnp.einsum('thc,uc->htu', query_codes, key_codes, preferred_element_type=...  4.22 us
    dot_general x6, matrix products, local(): jnp.einsum('htu,thc->uc', grad_scores, query_hat, preferred_element_type=...  4.01 us
  transfers between devices with their start and end apart: 25, of which 10 were waited for; matrix products, arithmetic and copies ran while one was open for 31% of the time, Pallas kernels for 0%

commit v1 on v0

v1 whole, which is shorter than its diff:
```python
import math

import jax
import jax.numpy as jnp
from jax import lax
from jax.experimental import pallas as pl
from jax.experimental.pallas import tpu as pltpu
from jax.sharding import PartitionSpec as P

AXES = ("row", "col")
SCALE_EPS = 1e-06
LOWEST = -3.0e38
TOP_LANE = 120
FACTOR_LANE = 121
DELTA_LANE = 122


def shifted(value, steps):
    count = lax.axis_size(AXES)
    first, last = max(0, -steps), min(count, count - steps)
    return lax.ppermute(value, AXES, [(source, source + steps) for source in range(first, last)])


def swapped(value, half):
    count = lax.axis_size(AXES)
    pairs = [(source, source + half if source % (2 * half) < half else source - half) for source in range(count)]
    return lax.ppermute(value, AXES, pairs)


def quantize(values):
    largest = jnp.max(jnp.abs(values), axis=-1, keepdims=True)
    scales = (largest + SCALE_EPS).astype(jnp.bfloat16).astype(jnp.float32)
    codes = jnp.clip(jnp.floor(values * (127.0 / scales) + 0.5), -127.0, 127.0)
    return codes, scales


def key_parts(keys):
    codes, scales = quantize(keys.astype(jnp.float32))
    exact = codes * scales
    high = exact.astype(jnp.bfloat16)
    low = (exact - high.astype(jnp.float32)).astype(jnp.bfloat16)
    return high, low


def dot_nt(left, right):
    return lax.dot_general(left, right, (((1,), (1,)), ((), ())), preferred_element_type=jnp.float32)


def dot_nn(left, right):
    return lax.dot_general(left, right, (((1,), (0,)), ((), ())), preferred_element_type=jnp.float32)


def dot_tn(left, right):
    return lax.dot_general(left, right, (((0,), (0,)), ((), ())), preferred_element_type=jnp.float32)


def with_ones(values):
    return jnp.concatenate([values, jnp.ones_like(values)], axis=1)


def lane_of(stats, lane):
    return stats[:, lane : lane + 1]


def put_lane(stats, lane, column):
    lanes = lax.broadcasted_iota(jnp.int32, stats.shape, 1)
    return jnp.where(lanes == lane, column, stats)


def level_scores(codes, key_pair):
    return dot_nt(jnp.concatenate([codes, codes], axis=1), key_pair)


def make_kernels(tokens, head, heads, levels):
    rows = tokens * heads
    tile = min(256, tokens)
    tiles = rows // tile
    score_factor = math.log2(math.e) / (127.0 * 127.0 * math.sqrt(head))
    score_scale = 1.0 / math.sqrt(head)
    vmem = pl.BlockSpec(memory_space=pltpu.VMEM)
    smem = pl.BlockSpec(memory_space=pltpu.SMEM)
    f32, bf16 = jnp.float32, jnp.bfloat16

    def own_forward(q_ref, kv_ref, codes_ref, hat_ref, w_ref, acc_ref, stats_ref):
        high, low = key_parts(kv_ref[:, :head])
        key_pair = jnp.concatenate([high, low], axis=1)
        values = with_ones(kv_ref[:, head:])
        for index in range(tiles):
            at = pl.ds(index * tile, tile)
            which, start = divmod(index * tile, tokens)
            raw = q_ref[pl.ds(start, tile), which * head : (which + 1) * head].astype(f32)
            codes, scales = quantize(raw)
            hat_ref[at, :] = (codes * (scales / 127.0)).astype(bf16)
            codes = codes.astype(bf16)
            codes_ref[at, :] = codes
            factor = scales * score_factor
            scores = level_scores(codes, key_pair)
            t = lax.broadcasted_iota(jnp.int32, scores.shape, 0) + start
            u = lax.broadcasted_iota(jnp.int32, scores.shape, 1)
            scores = jnp.where(u <= t, scores, LOWEST)
            top = jnp.max(scores, axis=1, keepdims=True)
            weights = jnp.exp2((scores - top) * factor).astype(bf16)
            w_ref[at, :] = weights
            acc_ref[at, :] = dot_nn(weights, values)
            stats = jnp.zeros((tile, 128), f32)
            stats = put_lane(stats, levels, top)
            stats = put_lane(stats, TOP_LANE, top)
            stats = put_lane(stats, FACTOR_LANE, factor)
            stats_ref[at, :] = stats

    def add_levels(which_levels, allowed_ref, codes, stats, acc, key_pairs, values, w_refs, at):
        factor = lane_of(stats, FACTOR_LANE)
        top = lane_of(stats, TOP_LANE)
        for level, key_pair, value, w_ref in zip(which_levels, key_pairs, values, w_refs):
            scores = level_scores(codes, key_pair)
            here = jnp.max(scores, axis=1, keepdims=True)
            weights = jnp.exp2((scores - here) * factor).astype(bf16)
            w_ref[at, :] = weights
            part = dot_nn(weights, value)
            allowed = allowed_ref[level] == 1
            new_top = jnp.maximum(top, jnp.where(allowed, here, LOWEST))
            grow = jnp.where(allowed, jnp.exp2((here - new_top) * factor), 0.0)
            acc = acc * jnp.exp2((top - new_top) * factor) + part * grow
            top = new_top
            stats = put_lane(stats, level, here)
        stats = put_lane(stats, TOP_LANE, top)
        return stats, acc

    def middle_forward(which_levels, allowed_ref, codes_ref, acc_in, stats_in, *refs):
        count = len(which_levels)
        kv_refs, w_refs = refs[:count], refs[count : 2 * count]
        acc_ref, stats_ref = refs[2 * count :]
        key_pairs = [jnp.concatenate(key_parts(kv[:, :head]), axis=1) for kv in kv_refs]
        values = [with_ones(kv[:, head:]) for kv in kv_refs]
        for index in range(tiles):
            at = pl.ds(index * tile, tile)
            stats, acc = add_levels(
                which_levels, allowed_ref, codes_ref[at, :], stats_in[at, :], acc_in[at, :], key_pairs, values, w_refs, at
            )
            stats_ref[at, :] = stats
            acc_ref[at, :] = acc

    def last_forward(which_levels, allowed_ref, codes_ref, acc_in, stats_in, grad_ref, *refs):
        count = len(which_levels)
        kv_refs, w_refs = refs[:count], refs[count : 2 * count]
        out_ref, stats_ref = refs[2 * count :]
        key_pairs = [jnp.concatenate(key_parts(kv[:, :head]), axis=1) for kv in kv_refs]
        values = [with_ones(kv[:, head:]) for kv in kv_refs]
        for index in range(tiles):
            at = pl.ds(index * tile, tile)
            which, start = divmod(index * tile, tokens)
            columns = slice(which * head, (which + 1) * head)
            stats, acc = add_levels(
                which_levels, allowed_ref, codes_ref[at, :], stats_in[at, :], acc_in[at, :], key_pairs, values, w_refs, at
            )
            inverse = 1.0 / acc[:, head : head + 1]
            mixed = (acc[:, :head] * inverse).astype(bf16)
            out_ref[pl.ds(start, tile), columns] = mixed
            grad = grad_ref[pl.ds(start, tile), columns].astype(f32)
            delta = jnp.sum(grad * mixed.astype(f32), axis=1, keepdims=True)
            top = lane_of(stats, TOP_LANE)
            factor = lane_of(stats, FACTOR_LANE)
            shares = jnp.exp2((stats - top) * factor) * inverse
            lanes = lax.broadcasted_iota(jnp.int32, shares.shape, 1)
            open_lanes = lanes == levels
            for level in range(levels):
                open_lanes = open_lanes | ((lanes == level) & (allowed_ref[level] == 1))
            shares = jnp.where(open_lanes, shares, 0.0)
            stats_ref[at, :] = put_lane(shares, DELTA_LANE, delta)

    def backward(which_levels, first, last, *refs):
        count = len(which_levels)
        hat_ref, grad_ref, stats_ref = refs[:3]
        refs = refs[3:]
        if not first:
            dq_in, refs = refs[0], refs[1:]
        kv_refs, w_refs = refs[:count], refs[count : 2 * count]
        dq_ref = refs[2 * count]
        part_refs = refs[2 * count + 1 :]
        highs = [key_parts(kv[:, :head])[0] for kv in kv_refs]
        values = [with_ones(kv[:, head:]) for kv in kv_refs]
        dk = [None] * count
        dv = [None] * count
        lanes = lax.broadcasted_iota(jnp.int32, (tile, head), 1)
        for index in range(tiles):
            at = pl.ds(index * tile, tile)
            which, start = divmod(index * tile, tokens)
            columns = slice(which * head, (which + 1) * head)
            grad = grad_ref[pl.ds(start, tile), columns].astype(f32)
            stats = stats_ref[at, :]
            delta = lane_of(stats, DELTA_LANE) * (-2.0 / head)
            hat = hat_ref[at, :]
            dq = None if first else dq_in[at, :]
            for place, level in enumerate(which_levels):
                share = lane_of(stats, level)
                shared_grad = (grad * share).astype(bf16)
                offset = delta * share
                coarse = offset.astype(bf16)
                fine = (offset - coarse.astype(f32)).astype(bf16)
                extra = jnp.where(lanes < head // 2, coarse, fine)
                weights = w_refs[place][at, :]
                moved = dot_nt(jnp.concatenate([shared_grad, extra], axis=1), values[place])
                grad_scores = (weights.astype(f32) * moved).astype(bf16)
                add_q = dot_nn(grad_scores, highs[place])
                add_k = dot_tn(grad_scores, hat)
                add_v = dot_tn(weights, shared_grad)
                dq = add_q if dq is None else dq + add_q
                dk[place] = add_k if dk[place] is None else dk[place] + add_k
                dv[place] = add_v if dv[place] is None else dv[place] + add_v
            if last:
                dq_ref[pl.ds(start, tile), columns] = (dq * (score_scale / 127.0)).astype(bf16)
            else:
                dq_ref[at, :] = dq
        for place, part_ref in enumerate(part_refs):
            part_ref[:, :head] = (dk[place] * score_scale).astype(part_ref.dtype)
            part_ref[:, head:] = dv[place].astype(part_ref.dtype)

    def shape(*dims, dtype=f32):
        return jax.ShapeDtypeStruct(dims, dtype)

    def call(body, name, in_specs, outs):
        return pl.pallas_call(
            body, name=name, in_specs=in_specs, out_specs=tuple(vmem for _ in outs), out_shape=tuple(outs)
        )

    wide, narrow = shape(rows, tokens, dtype=bf16), shape(rows, head, dtype=bf16)
    acc, stats = shape(rows, 2 * head), shape(rows, 128)
    flat = shape(tokens, heads * head, dtype=bf16)

    def run_own(q, kv):
        return call(own_forward, "own_forward", [vmem] * 2, [narrow, narrow, wide, acc, stats])(q, kv)

    def run_middle(which_levels, allowed, codes, acc_in, stats_in, kvs):
        count = len(which_levels)

        def body(*refs):
            middle_forward(which_levels, *refs)

        return call(body, "middle_forward", [smem] + [vmem] * (3 + count), [wide] * count + [acc, stats])(
            allowed, codes, acc_in, stats_in, *kvs
        )

    def run_last(which_levels, allowed, codes, acc_in, stats_in, grad, kvs):
        count = len(which_levels)

        def body(*refs):
            last_forward(which_levels, *refs)

        return call(body, "last_forward", [smem] + [vmem] * (4 + count), [wide] * count + [flat, stats])(
            allowed, codes, acc_in, stats_in, grad, *kvs
        )

    def run_backward(which_levels, hat, grad, stats_in, dq, kvs, ws, last=False, dtype=bf16):
        count = len(which_levels)
        first = dq is None

        def body(*refs):
            backward(which_levels, first, last, *refs)

        ins = [hat, grad, stats_in] + ([] if first else [dq]) + list(kvs) + list(ws)
        outs = [flat if last else shape(rows, head)] + [shape(tokens, 2 * head, dtype=dtype)] * count
        return call(body, "backward", [vmem] * len(ins), outs)(*ins)

    return run_own, run_middle, run_last, run_backward


def local(queries, key_rows, value_rows, out_grad, link_mask):
    tokens, head = key_rows.shape
    heads = queries.shape[1] // head
    levels = link_mask.shape[1]
    group = 2 ** (levels - 2)
    half = group // 2
    far, near, mid = levels - 1, levels - 2, levels - 3
    run_own, run_middle, run_last, run_backward = make_kernels(tokens, head, heads, levels)
    block = lax.axis_index(AXES)
    distances = 2 ** jnp.arange(levels, dtype=jnp.int32)
    allowed = jnp.where(block >= distances, link_mask[0], 0)
    upper = (block % group) >= half

    own = jnp.concatenate([key_rows, value_rows], axis=1)
    kv = {near: shifted(own, group)}
    for level in range(mid):
        kv[level] = shifted(own, 2**level)
    codes, hat, w_own, acc, stats = run_own(queries, own)
    kv[far] = shifted(kv[near], group)
    kv[mid] = swapped(jnp.where(upper, kv[near], own), half)
    w = {levels: w_own}
    early = [near] + list(range(mid))
    *ws, acc, stats = run_middle(early, allowed, codes, acc, stats, [kv[level] for level in early])
    w.update(zip(early, ws))
    late = [far, mid]
    *ws, attention_out, stats = run_last(late, allowed, codes, acc, stats, out_grad, [kv[level] for level in late])
    w.update(zip(late, ws))

    def step(which, dq, **options):
        kvs = [own if level == levels else kv[level] for level in which]
        return run_backward(which, hat, out_grad, stats, dq, kvs, [w[level] for level in which], **options)

    dq, part_far = step([far], None)
    got_far = shifted(part_far, -group)
    dq, part_mid = step([mid], dq)
    got_mid = swapped(part_mid, half)
    back = []
    for level in range(mid):
        dq, part = step([level], dq)
        back.append(shifted(part, -(2**level)))
    query_grad, part_near, part_own = step([near, levels], dq, last=True, dtype=jnp.float32)
    through = part_near + got_far.astype(jnp.float32)
    got_mid = got_mid.astype(jnp.float32)
    through = through + jnp.where(upper, got_mid, 0.0)
    got_near = shifted(through.astype(jnp.bfloat16), -group)
    total = part_own + jnp.where(upper, 0.0, got_mid) + got_near.astype(jnp.float32)
    for part in back:
        total = total + part.astype(jnp.float32)
    total = total.astype(jnp.bfloat16)
    return attention_out, query_grad, total[:, :head], total[:, head:]


def solution(mesh):
    spec = P(AXES, None)
    return jax.shard_map(local, mesh=mesh, in_specs=(spec,) * 5, out_specs=(spec,) * 4, check_vma=False)
```

time: 149 us -> 85.4 us (0.57); the launches traced: 146 us -> 84.8 us
  Pallas kernels: 0 us -> 42.9 us
  starting transfers between devices: 64.1 us -> 22.7 us
  matrix products: 28.3 us -> 0 us
  waiting for transfers between devices: 28.2 us -> 13.2 us
  other arithmetic: 13 us -> 1.92 us
  local copies, waits for them, and re-layouts: 8.05 us -> 3.32 us
  between operations: 4.77 us -> 0.85 us
    pallas_call x0 -> x8, Pallas kernels: none -> 42.9 us  [the longest x5 25.9 us: run_backward(): return call(body, 'backward', [vmem] * len(ins), outs)(*ins)]
    ppermute x25 -> x10, starting transfers between devices: 64.1 us -> 22.7 us  [the longest x8 19.4 us: shifted(): lax.ppermute(value, AXES, [(source, source + steps) for source in range(f...]
    dot_general x36 -> x0, matrix products: 28.3 us -> none  [the longest x6 6.06 us: local(): jnp.einsum('htu,thc->uc', probs.astype(jnp.bfloat16), grad_three, preferr...]
    ppermute x25 -> x10, waiting for transfers between devices: 28.2 us -> 13.2 us  [the longest x8 13.2 us: shifted(): lax.ppermute(value, AXES, [(source, source + steps) for source in range(f...]
    unnamed x45 -> x23, local copies, waits for them, and re-layouts: 7.29 us -> 2.56 us
    reduce_sum x2 -> x0, other arithmetic: 3.4 us -> none  [local(): total = total + jnp.sum(weights, axis=2)]
    add x7 -> x0, other arithmetic: 2.62 us -> none  [the longest x6 2.61 us: return_grads(): running = (running[0] + extra[0], running[1] + extra[1])]
    convert_element_type x9 -> x2, other arithmetic: 3.83 us -> 1.37 us  [the longest x1 1.2 us: local(): got_near = shifted(through.astype(jnp.bfloat16), -group)]
  transfers between devices with their start and end apart: 25 -> 10, of which waited for: 10 -> 2; matrix products, arithmetic and copies ran while one was open for 31% -> 2% of each run, Pallas kernels for 0% -> 32%
where the time goes in v1:
time: 85.4 us; the launch traced here: 84.8 us
  Pallas kernels  42.9 us (50%)
  starting transfers between devices  22.7 us (27%)
  waiting for transfers between devices  13.2 us (15%)
  local copies, waits for them, and re-layouts  3.32 us (4%)
  other arithmetic  1.92 us (2%)
    pallas_call x5, Pallas kernels, run_backward(): return call(body, 'backward', [vmem] * len(ins), outs)(*ins)  25.9 us
    ppermute x8, starting transfers between devices, shifted(): lax.ppermute(value, AXES, [(source, source + steps) for source in range(f...  19.4 us
    ppermute x8, waiting for transfers between devices, shifted(): lax.ppermute(value, AXES, [(source, source + steps) for source in range(f...  13.2 us
    pallas_call x1, Pallas kernels, run_middle(): call(body, 'middle_forward', [smem] + [vmem] * (3 + count), [wide] * coun...  7.02 us
    pallas_call x1, Pallas kernels, run_last(): call(body, 'last_forward', [smem] + [vmem] * (4 + count), [wide] * count...  6.26 us
    pallas_call x1, Pallas kernels, run_own(): call(own_forward, 'own_forward', [vmem] * 2, [narrow, narrow, wide, acc,...  3.72 us
    ppermute x2, starting transfers between devices, swapped(): return lax.ppermute(value, AXES, pairs)  3.28 us
    unnamed x23, local copies, waits for them, and re-layouts  2.56 us
  transfers between devices with their start and end apart: 10, of which 2 were waited for; matrix products, arithmetic and copies ran while one was open for 2% of the time, Pallas kernels for 32%

profile of v1, /device:TPU:0, one launch (start us, length us, event | category | flops | bytes accessed | tf_op | source)
XLA Modules:
  0.0 84.8 jit_solution(5524839444215509262)
XLA Ops:
  0.6 1.0 %constant_dynamic-update-slice_fusion.1 = bf16[512,256]{1,0:T(8,128)(2,1)S(1)} fusion(bf16[512,128]{1,0:T(8,128)(2,1)} %param.6), kind=kLoop, calls=%fused_computation.11 | loop fusion | bytes 262144
  1.7 5.0 %collective-permute-start = (bf16[512,256]{1,0:T(8,128)(2,1)S(1)}, bf16[512,256]{1,0:T(8,128)(2,1)S(1)}, u32[]{:S(2)}, u32[]{:S(2)}) collective-permute-start(bf16[512,256]{1,0:T(8,128)(2,1)S(1)} %constant_dynamic-update-slice_fusion.kv_ref.refs_5_), channel_id=1, source_target_pairs={{0,8},{1,9},{2,10},{3,11},{4,12},{5,13},{6,14},{7,15},{8,16},{9,17... | collective-permute-start | bytes 786440 | tf_op jit(solution)/shard_map/ppermute | solution.py:21
  6.6 1.5 %collective-permute-start.2 = (bf16[512,256]{1,0:T(8,128)(2,1)S(1)}, bf16[512,256]{1,0:T(8,128)(2,1)S(1)}, u32[]{:S(2)}, u32[]{:S(2)}) collective-permute-start(bf16[512,256]{1,0:T(8,128)(2,1)S(1)} %constant_dynamic-update-slice_fusion.kv_ref.refs_5_), channel_id=1, source_target_pairs={{0,2},{1,3},{2,4},{3,5},{4,6},{5,7},{6,8},{7,9},{8,10},{9,11},{10,... | collective-permute-start | bytes 786440 | tf_op jit(solution)/shard_map/ppermute | solution.py:21
  8.1 3.4 %collective-permute-start.1 = (bf16[512,256]{1,0:T(8,128)(2,1)S(1)}, bf16[512,256]{1,0:T(8,128)(2,1)S(1)}, u32[]{:S(2)}, u32[]{:S(2)}) collective-permute-start(bf16[512,256]{1,0:T(8,128)(2,1)S(1)} %constant_dynamic-update-slice_fusion.kv_ref.refs_5_), channel_id=1, source_target_pairs={{0,1},{1,2},{2,3},{3,4},{4,5},{5,6},{6,7},{7,8},{8,9},{9,10},{10,1... | collective-permute-start | bytes 786440 | tf_op jit(solution)/shard_map/ppermute | solution.py:21
  12.2 2.7 %collective-permute-start.4 = (bf16[512,256]{1,0:T(8,128)(2,1)S(1)}, bf16[512,256]{1,0:T(8,128)(2,1)S(1)}, u32[]{:S(2)}, u32[]{:S(2)}) collective-permute-start(bf16[512,256]{1,0:T(8,128)(2,1)S(1)} %broadcast_select_fusion), channel_id=1, source_target_pairs={{0,4},{1,5},{2,6},{3,7},{4,0},{5,1},{6,2},{7,3},{8,12},{9,13},{10,... | collective-permute-start | bytes 786440 | tf_op jit(solution)/shard_map/ppermute | solution.py:27
  14.9 4.4 %collective-permute-start.3 = (bf16[512,256]{1,0:T(8,128)(2,1)S(1)}, bf16[512,256]{1,0:T(8,128)(2,1)S(1)}, u32[]{:S(2)}, u32[]{:S(2)}) collective-permute-start(bf16[512,256]{1,0:T(8,128)(2,1)S(1)} %collective-permute-done.refs_4_), channel_id=1, source_target_pairs={{0,8},{1,9},{2,10},{3,11},{4,12},{5,13},{6,14},{7,15},{8,16},{9,17... | collective-permute-start | bytes 786440 | tf_op jit(solution)/shard_map/ppermute | solution.py:21
  19.3 3.7 %own_forward.1 = (bf16[1024,128]{1,0:T(8,128)(2,1)}, bf16[1024,128]{1,0:T(8,128)(2,1)}, bf16[1024,512]{1,0:T(8,128)(2,1)}, f32[1024,256]{1,0:T(8,128)}, f32[1024,128]{1,0:T(8,128)}) custom-call(bf16[512,256]{1,0:T(8,128)(2,1)} %q_ref.1, bf16[512,256]{1,0:T(8,128)(2,1)} %copy-done), custom_call_target="tpu_custom_call" | custom-call | tf_op jit(solution)/shard_map/own_forward/pallas_call | solution.py:231
  23.6 0.7 copy-done.3
  24.4 7.0 %middle_forward.1 = (bf16[1024,512]{1,0:T(8,128)(2,1)}, bf16[1024,512]{1,0:T(8,128)(2,1)}, bf16[1024,512]{1,0:T(8,128)(2,1)}, f32[1024,256]{1,0:T(8,128)}, f32[1024,128]{1,0:T(8,128)}) custom-call(s32[5]{0:T(128)} %compare_select_fusion.refs_0_, bf16[1024,128]{1,0:T(8,128)(2,1)} %get-tuple-element.29.refs_1_, f32[1024,256]{1,0:T(8,128)} %get-tuple-element.30.refs_2_, ...), custom_call_target="tpu_custom_call" | custom-call | tf_op jit(solution)/shard_map/middle_forward/pallas_call | solution.py:239
  31.4 0.7 copy-done.5
  32.2 6.3 %last_forward.1 = (bf16[1024,512]{1,0:T(8,128)(2,1)}, bf16[1024,512]{1,0:T(8,128)(2,1)}, bf16[512,256]{1,0:T(8,128)(2,1)}, f32[1024,128]{1,0:T(8,128)}) custom-call(s32[5]{0:T(128)} %compare_select_fusion.refs_0_, bf16[1024,128]{1,0:T(8,128)(2,1)} %get-tuple-element.29.refs_1_, f32[1024,256]{1,0:T(8,128)} %get-tuple-element.32.refs_2_, ...), custom_call_target="tpu_custom_call" | custom-call | tf_op jit(solution)/shard_map/last_forward/pallas_call | solution.py:249
  38.5 4.5 %backward.5 = (f32[1024,128]{1,0:T(8,128)}, bf16[512,256]{1,0:T(8,128)(2,1)}) custom-call(bf16[1024,128]{1,0:T(8,128)(2,1)} %get-tuple-element.35.refs_0_, bf16[512,256]{1,0:T(8,128)(2,1)} %refs_1_.9, f32[1024,128]{1,0:T(8,128)} %get-tuple-element.36.refs_2_, bf16[512,256]{1,0:T(8,128)(2,1)} %copy-done.2, bf16[1024,512]{1,0:T(8,128)(2,1)} %get-tuple-element.37.refs_4_), custom_call_target="tpu_custom_call" | custom-call | tf_op jit(solution)/shard_map/backward/pallas_call | solution.py:262
  42.9 4.7 %backward.6 = (f32[1024,128]{1,0:T(8,128)}, bf16[512,256]{1,0:T(8,128)(2,1)}) custom-call(bf16[1024,128]{1,0:T(8,128)(2,1)} %get-tuple-element.35.refs_0_, bf16[512,256]{1,0:T(8,128)(2,1)} %refs_1_.9, f32[1024,128]{1,0:T(8,128)} %get-tuple-element.36.refs_2_, f32[1024,128]{1,0:T(8,128)} %get-tuple-element.38.refs_3_, bf16[512,256]{1,0:T(8,128)(2,1)} %copy-done.5, ...), custom_call_target="tpu_custom_call" | custom-call | tf_op jit(solution)/shard_map/backward/pallas_call | solution.py:262
  47.7 0.6 collective-permute-start.5
  48.3 1.3 %collective-permute-start.6 = (bf16[512,256]{1,0:T(8,128)(2,1)S(1)}, bf16[512,256]{1,0:T(8,128)(2,1)S(1)}, u32[]{:S(2)}, u32[]{:S(2)}) collective-permute-start(bf16[512,256]{1,0:T(8,128)(2,1)S(1)} %copy-done.8), channel_id=1, source_target_pairs={{8,0},{9,1},{10,2},{11,3},{12,4},{13,5},{14,6},{15,7},{16,8},{17,9... | collective-permute-start | bytes 786440 | tf_op jit(solution)/shard_map/ppermute | solution.py:21
  49.6 4.6 %backward.7 = (f32[1024,128]{1,0:T(8,128)}, bf16[512,256]{1,0:T(8,128)(2,1)}) custom-call(bf16[1024,128]{1,0:T(8,128)(2,1)} %get-tuple-element.35.refs_0_, bf16[512,256]{1,0:T(8,128)(2,1)} %refs_1_.9, f32[1024,128]{1,0:T(8,128)} %get-tuple-element.36.refs_2_, f32[1024,128]{1,0:T(8,128)} %get-tuple-element.40.refs_3_, bf16[512,256]{1,0:T(8,128)(2,1)} %copy-done.4, ...), custom_call_target="tpu_custom_call" | custom-call | tf_op jit(solution)/shard_map/backward/pallas_call | solution.py:262
  54.2 4.7 %backward.8 = (f32[1024,128]{1,0:T(8,128)}, bf16[512,256]{1,0:T(8,128)(2,1)}) custom-call(bf16[1024,128]{1,0:T(8,128)(2,1)} %get-tuple-element.35.refs_0_, bf16[512,256]{1,0:T(8,128)(2,1)} %refs_1_.9, f32[1024,128]{1,0:T(8,128)} %get-tuple-element.36.refs_2_, f32[1024,128]{1,0:T(8,128)} %get-tuple-element.42.refs_3_, bf16[512,256]{1,0:T(8,128)(2,1)} %copy-done.3, ...), custom_call_target="tpu_custom_call" | custom-call | tf_op jit(solution)/shard_map/backward/pallas_call | solution.py:262
  58.9 1.3 %collective-permute-start.9 = (bf16[512,256]{1,0:T(8,128)(2,1)}, bf16[512,256]{1,0:T(8,128)(2,1)S(1)}, u32[]{:S(2)}, u32[]{:S(2)}) collective-permute-start(bf16[512,256]{1,0:T(8,128)(2,1)} %get-tuple-element.53), channel_id=1, source_target_pairs={{2,0},{3,1},{4,2},{5,3},{6,4},{7,5},{8,6},{9,7},{10,8},{11,9},{12,... | collective-permute-start | bytes 786440 | tf_op jit(solution)/shard_map/ppermute | solution.py:21
  60.2 1.3 %collective-permute-start.8 = (bf16[512,256]{1,0:T(8,128)(2,1)S(1)}, bf16[512,256]{1,0:T(8,128)(2,1)S(1)}, u32[]{:S(2)}, u32[]{:S(2)}) collective-permute-start(bf16[512,256]{1,0:T(8,128)(2,1)S(1)} %copy-done.9), channel_id=1, source_target_pairs={{1,0},{2,1},{3,2},{4,3},{5,4},{6,5},{7,6},{8,7},{9,8},{10,9},{11,1... | collective-permute-start | bytes 786440 | tf_op jit(solution)/shard_map/ppermute | solution.py:21
  61.5 7.3 %backward.9 = (bf16[512,256]{1,0:T(8,128)(2,1)}, f32[512,256]{1,0:T(8,128)}, f32[512,256]{1,0:T(8,128)}) custom-call(bf16[1024,128]{1,0:T(8,128)(2,1)} %get-tuple-element.35.refs_0_, bf16[512,256]{1,0:T(8,128)(2,1)} %refs_1_.9, f32[1024,128]{1,0:T(8,128)} %get-tuple-element.36.refs_2_, f32[1024,128]{1,0:T(8,128)} %get-tuple-element.44.refs_3_, ...), custom_call_target="tpu_custom_call" | custom-call | tf_op jit(solution)/shard_map/backward/pallas_call | solution.py:262
  68.8 1.2 %fusion.6 = bf16[512,256]{1,0:T(8,128)(2,1)S(1)} fusion(bf16[512,256]{1,0:T(8,128)(2,1)S(1)} %collective-permute-done.5, f32[512,256]{1,0:T(8,128)} %get-tuple-element.50, bf16[512,256]{1,0:T(8,128)(2,1)S(1)} %collective-permute-done.6, pred[]{:T(512)S(6)} %ge.11), kind=kLoop, calls=%fused_computation.8 | loop fusion | flops 786432 | bytes 1310721 | tf_op jit(solution)/shard_map/convert_element_type | solution.py:311
  70.1 1.3 %collective-permute-start.7 = (bf16[512,256]{1,0:T(8,128)(2,1)S(1)}, bf16[512,256]{1,0:T(8,128)(2,1)S(1)}, u32[]{:S(2)}, u32[]{:S(2)}) collective-permute-start(bf16[512,256]{1,0:T(8,128)(2,1)S(1)} %fusion.6), channel_id=1, source_target_pairs={{8,0},{9,1},{10,2},{11,3},{12,4},{13,5},{14,6},{15,7},{16,8},{17,9... | collective-permute-start | bytes 786440 | tf_op jit(solution)/shard_map/ppermute | solution.py:21
  71.4 12.6 %collective-permute-done.7 = bf16[512,256]{1,0:T(8,128)(2,1)S(1)} collective-permute-done((bf16[512,256]{1,0:T(8,128)(2,1)S(1)}, bf16[512,256]{1,0:T(8,128)(2,1)S(1)}, u32[]{:S(2)}, u32[]{:S(2)}) %collective-permute-start.7) | collective-permute-done | bytes 262176 | tf_op jit(solution)/shard_map/ppermute | solution.py:21
  84.1 0.7 fusion.9
  (33 shorter events, 1.6 us)
Async XLA Ops:
  0.6 1.0 %copy-start.7 = (bf16[512,128]{1,0:T(8,128)(2,1)S(1)}, bf16[512,128]{1,0:T(8,128)(2,1)}, u32[]{:S(2)}) copy-start(bf16[512,128]{1,0:T(8,128)(2,1)} %param.7) | copy-start | bytes 393220
  1.7 10.6 %copy-start = (bf16[512,256]{1,0:T(8,128)(2,1)}, bf16[512,256]{1,0:T(8,128)(2,1)S(1)}, u32[]{:S(2)}) copy-start(bf16[512,256]{1,0:T(8,128)(2,1)S(1)} %constant_dynamic-update-slice_fusion.kv_ref.refs_5_) | copy-start | bytes 786436
  1.7 10.5 %collective-permute-start = (bf16[512,256]{1,0:T(8,128)(2,1)S(1)}, bf16[512,256]{1,0:T(8,128)(2,1)S(1)}, u32[]{:S(2)}, u32[]{:S(2)}) collective-permute-start(bf16[512,256]{1,0:T(8,128)(2,1)S(1)} %constant_dynamic-update-slice_fusion.kv_ref.refs_5_), channel_id=1, source_target_pairs={{0,8},{1,9},{2,10},{3,11},{4,12},{5,13},{6,14},{7,15},{8,16},{9,17... | collective-permute-start | bytes 786440 | tf_op jit(solution)/shard_map/ppermute | solution.py:21
  6.6 16.9 %collective-permute-start.2 = (bf16[512,256]{1,0:T(8,128)(2,1)S(1)}, bf16[512,256]{1,0:T(8,128)(2,1)S(1)}, u32[]{:S(2)}, u32[]{:S(2)}) collective-permute-start(bf16[512,256]{1,0:T(8,128)(2,1)S(1)} %constant_dynamic-update-slice_fusion.kv_ref.refs_5_), channel_id=1, source_target_pairs={{0,2},{1,3},{2,4},{3,5},{4,6},{5,7},{6,8},{7,9},{8,10},{9,11},{10,... | collective-permute-start | bytes 786440 | tf_op jit(solution)/shard_map/ppermute | solution.py:21
  8.1 15.4 %collective-permute-start.1 = (bf16[512,256]{1,0:T(8,128)(2,1)S(1)}, bf16[512,256]{1,0:T(8,128)(2,1)S(1)}, u32[]{:S(2)}, u32[]{:S(2)}) collective-permute-start(bf16[512,256]{1,0:T(8,128)(2,1)S(1)} %constant_dynamic-update-slice_fusion.kv_ref.refs_5_), channel_id=1, source_target_pairs={{0,1},{1,2},{2,3},{3,4},{4,5},{5,6},{6,7},{7,8},{8,9},{9,10},{10,1... | collective-permute-start | bytes 786440 | tf_op jit(solution)/shard_map/ppermute | solution.py:21
  12.2 2.7 %copy-start.1 = (bf16[512,256]{1,0:T(8,128)(2,1)}, bf16[512,256]{1,0:T(8,128)(2,1)S(1)}, u32[]{:S(2)}) copy-start(bf16[512,256]{1,0:T(8,128)(2,1)S(1)} %collective-permute-done.refs_4_) | copy-start | bytes 786436
  12.2 10.8 %copy-start.10 = (s32[1,5]{1,0:T(1,128)S(1)}, s32[1,5]{1,0:T(1,128)}, u32[]{:S(2)}) copy-start(s32[1,5]{1,0:T(1,128)} %param.9) | copy-start | bytes 64
  12.2 19.2 %collective-permute-start.4 = (bf16[512,256]{1,0:T(8,128)(2,1)S(1)}, bf16[512,256]{1,0:T(8,128)(2,1)S(1)}, u32[]{:S(2)}, u32[]{:S(2)}) collective-permute-start(bf16[512,256]{1,0:T(8,128)(2,1)S(1)} %broadcast_select_fusion), channel_id=1, source_target_pairs={{0,4},{1,5},{2,6},{3,7},{4,0},{5,1},{6,2},{7,3},{8,12},{9,13},{10,... | collective-permute-start | bytes 786440 | tf_op jit(solution)/shard_map/ppermute | solution.py:27
  14.9 16.5 %collective-permute-start.3 = (bf16[512,256]{1,0:T(8,128)(2,1)S(1)}, bf16[512,256]{1,0:T(8,128)(2,1)S(1)}, u32[]{:S(2)}, u32[]{:S(2)}) collective-permute-start(bf16[512,256]{1,0:T(8,128)(2,1)S(1)} %collective-permute-done.refs_4_), channel_id=1, source_target_pairs={{0,8},{1,9},{2,10},{3,11},{4,12},{5,13},{6,14},{7,15},{8,16},{9,17... | collective-permute-start | bytes 786440 | tf_op jit(solution)/shard_map/ppermute | solution.py:21
  23.6 0.7 copy-start.3
  23.6 0.8 copy-start.4
  31.4 0.7 copy-start.5
  31.4 0.8 copy-start.2
  42.9 5.3 %copy-start.8 = (bf16[512,256]{1,0:T(8,128)(2,1)S(1)}, bf16[512,256]{1,0:T(8,128)(2,1)}, u32[]{:S(2)}) copy-start(bf16[512,256]{1,0:T(8,128)(2,1)} %get-tuple-element.51) | copy-start | bytes 786436
  47.7 21.2 %collective-permute-start.5 = (bf16[512,256]{1,0:T(8,128)(2,1)}, bf16[512,256]{1,0:T(8,128)(2,1)S(1)}, u32[]{:S(2)}, u32[]{:S(2)}) collective-permute-start(bf16[512,256]{1,0:T(8,128)(2,1)} %get-tuple-element.49), channel_id=1, source_target_pairs={{0,4},{1,5},{2,6},{3,7},{4,0},{5,1},{6,2},{7,3},{8,12},{9,13},{10,... | collective-permute-start | bytes 786440 | tf_op jit(solution)/shard_map/ppermute | solution.py:27
  48.3 20.6 %collective-permute-start.6 = (bf16[512,256]{1,0:T(8,128)(2,1)S(1)}, bf16[512,256]{1,0:T(8,128)(2,1)S(1)}, u32[]{:S(2)}, u32[]{:S(2)}) collective-permute-start(bf16[512,256]{1,0:T(8,128)(2,1)S(1)} %copy-done.8), channel_id=1, source_target_pairs={{8,0},{9,1},{10,2},{11,3},{12,4},{13,5},{14,6},{15,7},{16,8},{17,9... | collective-permute-start | bytes 786440 | tf_op jit(solution)/shard_map/ppermute | solution.py:21
  54.2 6.0 %copy-start.9 = (bf16[512,256]{1,0:T(8,128)(2,1)S(1)}, bf16[512,256]{1,0:T(8,128)(2,1)}, u32[]{:S(2)}) copy-start(bf16[512,256]{1,0:T(8,128)(2,1)} %get-tuple-element.52) | copy-start | bytes 786436
  58.9 12.5 %collective-permute-start.9 = (bf16[512,256]{1,0:T(8,128)(2,1)}, bf16[512,256]{1,0:T(8,128)(2,1)S(1)}, u32[]{:S(2)}, u32[]{:S(2)}) collective-permute-start(bf16[512,256]{1,0:T(8,128)(2,1)} %get-tuple-element.53), channel_id=1, source_target_pairs={{2,0},{3,1},{4,2},{5,3},{6,4},{7,5},{8,6},{9,7},{10,8},{11,9},{12,... | collective-permute-start | bytes 786440 | tf_op jit(solution)/shard_map/ppermute | solution.py:21
  60.2 11.2 %collective-permute-start.8 = (bf16[512,256]{1,0:T(8,128)(2,1)S(1)}, bf16[512,256]{1,0:T(8,128)(2,1)S(1)}, u32[]{:S(2)}, u32[]{:S(2)}) collective-permute-start(bf16[512,256]{1,0:T(8,128)(2,1)S(1)} %copy-done.9), channel_id=1, source_target_pairs={{1,0},{2,1},{3,2},{4,3},{5,4},{6,5},{7,6},{8,7},{9,8},{10,9},{11,1... | collective-permute-start | bytes 786440 | tf_op jit(solution)/shard_map/ppermute | solution.py:21
  68.8 15.1 %copy-start.6 = (f32[512,256]{1,0:T(8,128)S(1)}, f32[512,256]{1,0:T(8,128)}, u32[]{:S(2)}) copy-start(f32[512,256]{1,0:T(8,128)} %get-tuple-element.48) | copy-start | bytes 1572868
  70.1 13.9 %collective-permute-start.7 = (bf16[512,256]{1,0:T(8,128)(2,1)S(1)}, bf16[512,256]{1,0:T(8,128)(2,1)S(1)}, u32[]{:S(2)}, u32[]{:S(2)}) collective-permute-start(bf16[512,256]{1,0:T(8,128)(2,1)S(1)} %fusion.6), channel_id=1, source_target_pairs={{8,0},{9,1},{10,2},{11,3},{12,4},{13,5},{14,6},{15,7},{16,8},{17,9... | collective-permute-start | bytes 786440 | tf_op jit(solution)/shard_map/ppermute | solution.py:21

commit v2 on v1

--- a/solution.py
+++ b/solution.py
@@ -219,9 +219,24 @@
         return jax.ShapeDtypeStruct(dims, dtype)
 
     def call(body, name, in_specs, outs):
-        return pl.pallas_call(
-            body, name=name, in_specs=in_specs, out_specs=tuple(vmem for _ in outs), out_shape=tuple(outs)
+        run = pl.pallas_call(
+            body,
+            name=name,
+            in_specs=in_specs,
+            out_specs=tuple(vmem for _ in outs),
+            out_shape=tuple(pltpu.VMEM(out.shape, out.dtype) for out in outs),
+            compiler_params=pltpu.CompilerParams(vmem_limit_bytes=16 * 2**20),
         )
+
+        def placed(*operands):
+            return run(
+                *(
+                    pltpu.with_memory_space_constraint(operand, pltpu.VMEM) if spec is vmem else operand
+                    for spec, operand in zip(in_specs, operands)
+                )
+            )
+
+        return placed
 
     wide, narrow = shape(rows, tokens, dtype=bf16), shape(rows, head, dtype=bf16)
     acc, stats = shape(rows, 2 * head), shape(rows, 128)

time: 85.4 us -> 62 us (0.73)
  Pallas kernels: 42.9 us -> 22.9 us
  other arithmetic: 1.92 us -> 0.34 us
  waiting for transfers between devices: 13.2 us -> 12.1 us
    pallas_call x8, Pallas kernels: 42.9 us -> 22.9 us  [placed(): run(*(pltpu.with_memory_space_constraint(operand, pltpu.VMEM) if spec is...]
    ppermute x8, waiting for transfers between devices: 13.2 us -> 12.1 us  [shifted(): lax.ppermute(value, AXES, [(source, source + steps) for source in range(f...]
    convert_element_type x1, other arithmetic: 1.2 us -> 0.11 us  [local(): got_near = shifted(through.astype(jnp.bfloat16), -group)]
    unnamed x23 -> x11, local copies, waits for them, and re-layouts: 2.56 us -> 2.39 us
  transfers between devices with their start and end apart: 10 -> 10, of which waited for: 2 -> 3; matrix products, arithmetic and copies ran while one was open for 2% -> 3% of each run, Pallas kernels for 32% -> 23%
where the time goes in v2:
time: 62 us; the launch traced here: 61.7 us
  Pallas kernels  22.9 us (37%)
  starting transfers between devices  22.4 us (36%)
  waiting for transfers between devices  12.1 us (20%)
  local copies, waits for them, and re-layouts  3.15 us (5%)
  between operations  0.89 us (1%)
    pallas_call x8, Pallas kernels, placed(): run(*(pltpu.with_memory_space_constraint(operand, pltpu.VMEM) if spec is...  22.9 us
    ppermute x8, starting transfers between devices, shifted(): lax.ppermute(value, AXES, [(source, source + steps) for source in range(f...  19.6 us
    ppermute x8, waiting for transfers between devices, shifted(): lax.ppermute(value, AXES, [(source, source + steps) for source in range(f...  12.1 us
    ppermute x2, starting transfers between devices, swapped(): return lax.ppermute(value, AXES, pairs)  2.78 us
    unnamed x11, local copies, waits for them, and re-layouts  2.39 us
  transfers between devices with their start and end apart: 10, of which 3 were waited for; matrix products, arithmetic and copies ran while one was open for 3% of the time, Pallas kernels for 23%

profile of v2, /device:TPU:0, one launch (start us, length us, event | category | flops | bytes accessed | tf_op | source)
XLA Modules:
  0.0 61.7 jit_solution(9216791583975860623)
XLA Ops:
  0.6 1.0 %constant_dynamic-update-slice_fusion.1 = bf16[512,256]{1,0:T(8,128)(2,1)S(1)} fusion(bf16[512,128]{1,0:T(8,128)(2,1)} %param.6), kind=kLoop, calls=%fused_computation.11 | loop fusion | bytes 262144
  1.7 5.0 %collective-permute-start = (bf16[512,256]{1,0:T(8,128)(2,1)S(1)}, bf16[512,256]{1,0:T(8,128)(2,1)S(1)}, u32[]{:S(2)}, u32[]{:S(2)}) collective-permute-start(bf16[512,256]{1,0:T(8,128)(2,1)S(1)} %constant_dynamic-update-slice_fusion.kv_ref.refs_5_), channel_id=1, source_target_pairs={{0,8},{1,9},{2,10},{3,11},{4,12},{5,13},{6,14},{7,15},{8,16},{9,17... | collective-permute-start | bytes 786440 | tf_op jit(solution)/shard_map/ppermute | solution.py:21
  6.6 1.5 %collective-permute-start.2 = (bf16[512,256]{1,0:T(8,128)(2,1)S(1)}, bf16[512,256]{1,0:T(8,128)(2,1)S(1)}, u32[]{:S(2)}, u32[]{:S(2)}) collective-permute-start(bf16[512,256]{1,0:T(8,128)(2,1)S(1)} %constant_dynamic-update-slice_fusion.kv_ref.refs_5_), channel_id=1, source_target_pairs={{0,2},{1,3},{2,4},{3,5},{4,6},{5,7},{6,8},{7,9},{8,10},{9,11},{10,... | collective-permute-start | bytes 786440 | tf_op jit(solution)/shard_map/ppermute | solution.py:21
  8.1 3.4 %collective-permute-start.1 = (bf16[512,256]{1,0:T(8,128)(2,1)S(1)}, bf16[512,256]{1,0:T(8,128)(2,1)S(1)}, u32[]{:S(2)}, u32[]{:S(2)}) collective-permute-start(bf16[512,256]{1,0:T(8,128)(2,1)S(1)} %constant_dynamic-update-slice_fusion.kv_ref.refs_5_), channel_id=1, source_target_pairs={{0,1},{1,2},{2,3},{3,4},{4,5},{5,6},{6,7},{7,8},{8,9},{9,10},{10,1... | collective-permute-start | bytes 786440 | tf_op jit(solution)/shard_map/ppermute | solution.py:21
  11.6 0.6 collective-permute-done.refs_4_
  12.2 2.7 %collective-permute-start.4 = (bf16[512,256]{1,0:T(8,128)(2,1)S(1)}, bf16[512,256]{1,0:T(8,128)(2,1)S(1)}, u32[]{:S(2)}, u32[]{:S(2)}) collective-permute-start(bf16[512,256]{1,0:T(8,128)(2,1)S(1)} %broadcast_select_fusion), channel_id=1, source_target_pairs={{0,4},{1,5},{2,6},{3,7},{4,0},{5,1},{6,2},{7,3},{8,12},{9,13},{10,... | collective-permute-start | bytes 786440 | tf_op jit(solution)/shard_map/ppermute | solution.py:27
  14.9 4.4 %collective-permute-start.3 = (bf16[512,256]{1,0:T(8,128)(2,1)S(1)}, bf16[512,256]{1,0:T(8,128)(2,1)S(1)}, u32[]{:S(2)}, u32[]{:S(2)}) collective-permute-start(bf16[512,256]{1,0:T(8,128)(2,1)S(1)} %collective-permute-done.refs_4_), channel_id=1, source_target_pairs={{0,8},{1,9},{2,10},{3,11},{4,12},{5,13},{6,14},{7,15},{8,16},{9,17... | collective-permute-start | bytes 786440 | tf_op jit(solution)/shard_map/ppermute | solution.py:21
  19.3 1.4 %own_forward.1 = (bf16[1024,128]{1,0:T(8,128)(2,1)S(1)}, bf16[1024,128]{1,0:T(8,128)(2,1)S(1)}, bf16[1024,512]{1,0:T(8,128)(2,1)S(1)}, f32[1024,256]{1,0:T(8,128)S(1)}, f32[1024,128]{1,0:T(8,128)S(1)}) custom-call(bf16[512,256]{1,0:T(8,128)(2,1)S(1)} %copy-done.1, bf16[512,256]{1,0:T(8,128)(2,1)S(1)} %constant_dynamic-update-slice_fusion.kv_ref.refs_5_), custom_call_target="tpu_custom_call" | custom-call | tf_op jit(solution)/shard_map/own_forward/pallas_call | solution.py:232
  20.7 4.3 %middle_forward.1 = (bf16[1024,512]{1,0:T(8,128)(2,1)S(1)}, bf16[1024,512]{1,0:T(8,128)(2,1)S(1)}, bf16[1024,512]{1,0:T(8,128)(2,1)S(1)}, f32[1024,256]{1,0:T(8,128)S(1)}, f32[1024,128]{1,0:T(8,128)S(1)}) custom-call(s32[5]{0:T(128)S(1)} %compare_select_fusion.refs_0_, bf16[1024,128]{1,0:T(8,128)(2,1)S(1)} %get-tuple-element.29.refs_1_, ...), custom_call_target="tpu_custom_call" | custom-call | tf_op jit(solution)/shard_map/middle_forward/pallas_call | solution.py:232
  25.1 4.2 %last_forward.1 = (bf16[1024,512]{1,0:T(8,128)(2,1)S(1)}, bf16[1024,512]{1,0:T(8,128)(2,1)S(1)}, bf16[512,256]{1,0:T(8,128)(2,1)S(1)}, f32[1024,128]{1,0:T(8,128)S(1)}) custom-call(s32[5]{0:T(128)S(1)} %compare_select_fusion.refs_0_, bf16[1024,128]{1,0:T(8,128)(2,1)S(1)} %get-tuple-element.29.refs_1_, f32[1024,256]{1,0:T(8,128)S(1)} %get-tuple-element.32.refs_2_, ...), custom_call_target="tpu_custom_call" | custom-call | tf_op jit(solution)/shard_map/last_forward/pallas_call | solution.py:232
  29.4 2.1 %backward.5 = (f32[1024,128]{1,0:T(8,128)S(1)}, bf16[512,256]{1,0:T(8,128)(2,1)S(1)}) custom-call(bf16[1024,128]{1,0:T(8,128)(2,1)S(1)} %get-tuple-element.35.refs_0_, bf16[512,256]{1,0:T(8,128)(2,1)S(1)} %copy-done, f32[1024,128]{1,0:T(8,128)S(1)} %get-tuple-element.36.refs_2_, bf16[512,256]{1,0:T(8,128)(2,1)S(1)} %collective-permute-done.3.refs_5_.refs_3_, ...), custom_call_target="tpu_custom_call" | custom-call | tf_op jit(solution)/shard_map/backward/pallas_call | solution.py:232
  31.5 2.1 %backward.6 = (f32[1024,128]{1,0:T(8,128)S(1)}, bf16[512,256]{1,0:T(8,128)(2,1)S(1)}) custom-call(bf16[1024,128]{1,0:T(8,128)(2,1)S(1)} %get-tuple-element.35.refs_0_, bf16[512,256]{1,0:T(8,128)(2,1)S(1)} %copy-done, f32[1024,128]{1,0:T(8,128)S(1)} %get-tuple-element.36.refs_2_, f32[1024,128]{1,0:T(8,128)S(1)} %get-tuple-element.38.refs_3_, ...), custom_call_target="tpu_custom_call" | custom-call | tf_op jit(solution)/shard_map/backward/pallas_call | solution.py:232
  33.7 1.5 %collective-permute-start.6 = (bf16[512,256]{1,0:T(8,128)(2,1)S(1)}, bf16[512,256]{1,0:T(8,128)(2,1)S(1)}, u32[]{:S(2)}, u32[]{:S(2)}) collective-permute-start(bf16[512,256]{1,0:T(8,128)(2,1)S(1)} %get-tuple-element.51), channel_id=1, source_target_pairs={{8,0},{9,1},{10,2},{11,3},{12,4},{13,5},{14,6},{15,7},{16,8},{17,9... | collective-permute-start | bytes 786440 | tf_op jit(solution)/shard_map/ppermute | solution.py:21
  35.2 2.1 %backward.7 = (f32[1024,128]{1,0:T(8,128)S(1)}, bf16[512,256]{1,0:T(8,128)(2,1)S(1)}) custom-call(bf16[1024,128]{1,0:T(8,128)(2,1)S(1)} %get-tuple-element.35.refs_0_, bf16[512,256]{1,0:T(8,128)(2,1)S(1)} %copy-done, f32[1024,128]{1,0:T(8,128)S(1)} %get-tuple-element.36.refs_2_, f32[1024,128]{1,0:T(8,128)S(1)} %get-tuple-element.40.refs_3_, ...), custom_call_target="tpu_custom_call" | custom-call | tf_op jit(solution)/shard_map/backward/pallas_call | solution.py:232
  37.4 2.1 %backward.8 = (f32[1024,128]{1,0:T(8,128)S(1)}, bf16[512,256]{1,0:T(8,128)(2,1)S(1)}) custom-call(bf16[1024,128]{1,0:T(8,128)(2,1)S(1)} %get-tuple-element.35.refs_0_, bf16[512,256]{1,0:T(8,128)(2,1)S(1)} %copy-done, f32[1024,128]{1,0:T(8,128)S(1)} %get-tuple-element.36.refs_2_, f32[1024,128]{1,0:T(8,128)S(1)} %get-tuple-element.42.refs_3_, ...), custom_call_target="tpu_custom_call" | custom-call | tf_op jit(solution)/shard_map/backward/pallas_call | solution.py:232
  39.5 1.3 %collective-permute-start.9 = (bf16[512,256]{1,0:T(8,128)(2,1)S(1)}, bf16[512,256]{1,0:T(8,128)(2,1)S(1)}, u32[]{:S(2)}, u32[]{:S(2)}) collective-permute-start(bf16[512,256]{1,0:T(8,128)(2,1)S(1)} %get-tuple-element.53), channel_id=1, source_target_pairs={{2,0},{3,1},{4,2},{5,3},{6,4},{7,5},{8,6},{9,7},{10,8},{11,9},{12,... | collective-permute-start | bytes 786440 | tf_op jit(solution)/shard_map/ppermute | solution.py:21
  40.8 1.3 %collective-permute-start.8 = (bf16[512,256]{1,0:T(8,128)(2,1)S(1)}, bf16[512,256]{1,0:T(8,128)(2,1)S(1)}, u32[]{:S(2)}, u32[]{:S(2)}) collective-permute-start(bf16[512,256]{1,0:T(8,128)(2,1)S(1)} %get-tuple-element.52), channel_id=1, source_target_pairs={{1,0},{2,1},{3,2},{4,3},{5,4},{6,5},{7,6},{8,7},{9,8},{10,9},{11,1... | collective-permute-start | bytes 786440 | tf_op jit(solution)/shard_map/ppermute | solution.py:21
  42.1 4.3 %backward.9 = (bf16[512,256]{1,0:T(8,128)(2,1)S(1)}, f32[512,256]{1,0:T(8,128)S(1)}, f32[512,256]{1,0:T(8,128)S(1)}) custom-call(bf16[1024,128]{1,0:T(8,128)(2,1)S(1)} %get-tuple-element.35.refs_0_, bf16[512,256]{1,0:T(8,128)(2,1)S(1)} %copy-done, f32[1024,128]{1,0:T(8,128)S(1)} %get-tuple-element.36.refs_2_, f32[1024,128]{1,0:T(8,128)S(1)} %get-tuple-element.44.refs_3_, ...), custom_call_target="tpu_custom_call" | custom-call | tf_op jit(solution)/shard_map/backward/pallas_call | solution.py:232
  46.6 1.3 %collective-permute-start.7 = (bf16[512,256]{1,0:T(8,128)(2,1)S(1)}, bf16[512,256]{1,0:T(8,128)(2,1)S(1)}, u32[]{:S(2)}, u32[]{:S(2)}) collective-permute-start(bf16[512,256]{1,0:T(8,128)(2,1)S(1)} %fusion.6), channel_id=1, source_target_pairs={{8,0},{9,1},{10,2},{11,3},{12,4},{13,5},{14,6},{15,7},{16,8},{17,9... | collective-permute-start | bytes 786440 | tf_op jit(solution)/shard_map/ppermute | solution.py:21
  47.9 0.7 %copy.10 = bf16[512,256]{1,0:T(8,128)(2,1)} copy(bf16[512,256]{1,0:T(8,128)(2,1)S(1)} %get-tuple-element.56) | data formatting | bytes 524288
  48.6 0.7 %copy.11 = bf16[512,256]{1,0:T(8,128)(2,1)} copy(bf16[512,256]{1,0:T(8,128)(2,1)S(1)} %get-tuple-element.57) | data formatting | bytes 524288
  49.3 1.5 %collective-permute-done.8 = bf16[512,256]{1,0:T(8,128)(2,1)S(1)} collective-permute-done((bf16[512,256]{1,0:T(8,128)(2,1)S(1)}, bf16[512,256]{1,0:T(8,128)(2,1)S(1)}, u32[]{:S(2)}, u32[]{:S(2)}) %collective-permute-start.8) | collective-permute-done | bytes 262176 | tf_op jit(solution)/shard_map/ppermute | solution.py:21
  50.8 10.0 %collective-permute-done.7 = bf16[512,256]{1,0:T(8,128)(2,1)S(1)} collective-permute-done((bf16[512,256]{1,0:T(8,128)(2,1)S(1)}, bf16[512,256]{1,0:T(8,128)(2,1)S(1)}, u32[]{:S(2)}, u32[]{:S(2)}) %collective-permute-start.7) | collective-permute-done | bytes 262176 | tf_op jit(solution)/shard_map/ppermute | solution.py:21
  61.0 0.7 %fusion.9 = (bf16[512,128]{1,0:T(8,128)(2,1)}, bf16[512,128]{1,0:T(8,128)(2,1)}) fusion(bf16[512,256]{1,0:T(8,128)(2,1)S(1)} %fusion.4), kind=kLoop, calls=%fused_computation.23 | loop fusion | bytes 524288 | tf_op jit(solution)/shard_map/slice | solution.py:331
  (21 shorter events, 0.5 us)
Async XLA Ops:
  0.6 1.0 %copy-start.2 = (bf16[512,128]{1,0:T(8,128)(2,1)S(1)}, bf16[512,128]{1,0:T(8,128)(2,1)}, u32[]{:S(2)}) copy-start(bf16[512,128]{1,0:T(8,128)(2,1)} %param.7) | copy-start | bytes 393220
  1.7 10.5 %collective-permute-start = (bf16[512,256]{1,0:T(8,128)(2,1)S(1)}, bf16[512,256]{1,0:T(8,128)(2,1)S(1)}, u32[]{:S(2)}, u32[]{:S(2)}) collective-permute-start(bf16[512,256]{1,0:T(8,128)(2,1)S(1)} %constant_dynamic-update-slice_fusion.kv_ref.refs_5_), channel_id=1, source_target_pairs={{0,8},{1,9},{2,10},{3,11},{4,12},{5,13},{6,14},{7,15},{8,16},{9,17... | collective-permute-start | bytes 786440 | tf_op jit(solution)/shard_map/ppermute | solution.py:21
  6.6 14.1 %collective-permute-start.2 = (bf16[512,256]{1,0:T(8,128)(2,1)S(1)}, bf16[512,256]{1,0:T(8,128)(2,1)S(1)}, u32[]{:S(2)}, u32[]{:S(2)}) collective-permute-start(bf16[512,256]{1,0:T(8,128)(2,1)S(1)} %constant_dynamic-update-slice_fusion.kv_ref.refs_5_), channel_id=1, source_target_pairs={{0,2},{1,3},{2,4},{3,5},{4,6},{5,7},{6,8},{7,9},{8,10},{9,11},{10,... | collective-permute-start | bytes 786440 | tf_op jit(solution)/shard_map/ppermute | solution.py:21
  8.1 12.6 %collective-permute-start.1 = (bf16[512,256]{1,0:T(8,128)(2,1)S(1)}, bf16[512,256]{1,0:T(8,128)(2,1)S(1)}, u32[]{:S(2)}, u32[]{:S(2)}) collective-permute-start(bf16[512,256]{1,0:T(8,128)(2,1)S(1)} %constant_dynamic-update-slice_fusion.kv_ref.refs_5_), channel_id=1, source_target_pairs={{0,1},{1,2},{2,3},{3,4},{4,5},{5,6},{6,7},{7,8},{8,9},{9,10},{10,1... | collective-permute-start | bytes 786440 | tf_op jit(solution)/shard_map/ppermute | solution.py:21
  11.6 7.7 %copy-start.1 = (bf16[512,256]{1,0:T(8,128)(2,1)S(1)}, bf16[512,256]{1,0:T(8,128)(2,1)}, u32[]{:S(2)}) copy-start(bf16[512,256]{1,0:T(8,128)(2,1)} %q_ref.1) | copy-start | bytes 786436
  12.2 8.5 %copy-start.3 = (s32[1,5]{1,0:T(1,128)S(1)}, s32[1,5]{1,0:T(1,128)}, u32[]{:S(2)}) copy-start(s32[1,5]{1,0:T(1,128)} %param.9) | copy-start | bytes 64
  12.2 12.9 %collective-permute-start.4 = (bf16[512,256]{1,0:T(8,128)(2,1)S(1)}, bf16[512,256]{1,0:T(8,128)(2,1)S(1)}, u32[]{:S(2)}, u32[]{:S(2)}) collective-permute-start(bf16[512,256]{1,0:T(8,128)(2,1)S(1)} %broadcast_select_fusion), channel_id=1, source_target_pairs={{0,4},{1,5},{2,6},{3,7},{4,0},{5,1},{6,2},{7,3},{8,12},{9,13},{10,... | collective-permute-start | bytes 786440 | tf_op jit(solution)/shard_map/ppermute | solution.py:27
  14.9 10.2 %collective-permute-start.3 = (bf16[512,256]{1,0:T(8,128)(2,1)S(1)}, bf16[512,256]{1,0:T(8,128)(2,1)S(1)}, u32[]{:S(2)}, u32[]{:S(2)}) collective-permute-start(bf16[512,256]{1,0:T(8,128)(2,1)S(1)} %collective-permute-done.refs_4_), channel_id=1, source_target_pairs={{0,8},{1,9},{2,10},{3,11},{4,12},{5,13},{6,14},{7,15},{8,16},{9,17... | collective-permute-start | bytes 786440 | tf_op jit(solution)/shard_map/ppermute | solution.py:21
  20.7 4.4 %copy-start = (bf16[512,256]{1,0:T(8,128)(2,1)S(1)}, bf16[512,256]{1,0:T(8,128)(2,1)}, u32[]{:S(2)}) copy-start(bf16[512,256]{1,0:T(8,128)(2,1)} %refs_1_.9) | copy-start | bytes 786436
  33.7 12.8 %collective-permute-start.5 = (bf16[512,256]{1,0:T(8,128)(2,1)S(1)}, bf16[512,256]{1,0:T(8,128)(2,1)S(1)}, u32[]{:S(2)}, u32[]{:S(2)}) collective-permute-start(bf16[512,256]{1,0:T(8,128)(2,1)S(1)} %get-tuple-element.49), channel_id=1, source_target_pairs={{0,4},{1,5},{2,6},{3,7},{4,0},{5,1},{6,2},{7,3},{8,12},{9,13},{10,... | collective-permute-start | bytes 786440 | tf_op jit(solution)/shard_map/ppermute | solution.py:27
  33.7 12.7 %collective-permute-start.6 = (bf16[512,256]{1,0:T(8,128)(2,1)S(1)}, bf16[512,256]{1,0:T(8,128)(2,1)S(1)}, u32[]{:S(2)}, u32[]{:S(2)}) collective-permute-start(bf16[512,256]{1,0:T(8,128)(2,1)S(1)} %get-tuple-element.51), channel_id=1, source_target_pairs={{8,0},{9,1},{10,2},{11,3},{12,4},{13,5},{14,6},{15,7},{16,8},{17,9... | collective-permute-start | bytes 786440 | tf_op jit(solution)/shard_map/ppermute | solution.py:21
  39.5 9.8 %collective-permute-start.9 = (bf16[512,256]{1,0:T(8,128)(2,1)S(1)}, bf16[512,256]{1,0:T(8,128)(2,1)S(1)}, u32[]{:S(2)}, u32[]{:S(2)}) collective-permute-start(bf16[512,256]{1,0:T(8,128)(2,1)S(1)} %get-tuple-element.53), channel_id=1, source_target_pairs={{2,0},{3,1},{4,2},{5,3},{6,4},{7,5},{8,6},{9,7},{10,8},{11,9},{12,... | collective-permute-start | bytes 786440 | tf_op jit(solution)/shard_map/ppermute | solution.py:21
  40.8 10.0 %collective-permute-start.8 = (bf16[512,256]{1,0:T(8,128)(2,1)S(1)}, bf16[512,256]{1,0:T(8,128)(2,1)S(1)}, u32[]{:S(2)}, u32[]{:S(2)}) collective-permute-start(bf16[512,256]{1,0:T(8,128)(2,1)S(1)} %get-tuple-element.52), channel_id=1, source_target_pairs={{1,0},{2,1},{3,2},{4,3},{5,4},{6,5},{7,6},{8,7},{9,8},{10,9},{11,1... | collective-permute-start | bytes 786440 | tf_op jit(solution)/shard_map/ppermute | solution.py:21
  46.6 14.2 %collective-permute-start.7 = (bf16[512,256]{1,0:T(8,128)(2,1)S(1)}, bf16[512,256]{1,0:T(8,128)(2,1)S(1)}, u32[]{:S(2)}, u32[]{:S(2)}) collective-permute-start(bf16[512,256]{1,0:T(8,128)(2,1)S(1)} %fusion.6), channel_id=1, source_target_pairs={{8,0},{9,1},{10,2},{11,3},{12,4},{13,5},{14,6},{15,7},{16,8},{17,9... | collective-permute-start | bytes 786440 | tf_op jit(solution)/shard_map/ppermute | solution.py:21
